TPU v7x, 256 devices: a whole 4x4x8 slice. The times are simulated.
256 devices in a mesh: dp: 2 (over core), row: 16 (over y, x), col: 8 (over z).
Axes of the slice: x: 4, y: 4, z: 8, core: 2. Of those that a mesh axis runs over, the one named last changes fastest.
Arguments:
- features: bfloat16 [2, 256, 128, 1024], P('dp', None, 'row', 'col'), may hold values from -41 to 41, as said below
- group_kernel: bfloat16 [256, 72], replicated, may hold values from -0.75 to 0.75
- norm_gain: float32 [256], replicated, may hold values from 0.1 to 1.9
- norm_bias: float32 [256], replicated, may hold values from -3 to 3
- mix_weight: bfloat16 [256, 256], replicated, may hold values from -0.375 to 0.375
- cotangent: bfloat16 [2, 256, 128, 1024], P('dp', None, 'row', 'col'), may hold values from -6 to 6
Outputs:
- mixed: bfloat16 [2, 256, 128, 1024], P('dp', None, 'row', 'col')
- grad_features: bfloat16 [2, 256, 128, 1024], P('dp', None, 'row', 'col')
- grad_mix: float32 [256, 256], replicated
- grad_gain: float32 [256], replicated
- grad_bias: float32 [256], replicated
- grad_kernel: float32 [256, 72], replicated
- grad_whiten: float32 [2, 256, 256], P('dp')
Inputs may be any that keep to these rules, and one draw needn't show every extreme that they name: `features`: feature maps whose scale varies over channels and over cells.
All inputs are finite; a program needn't handle non-finite values.
Results may differ from a plain program's by a relative error of at most 0.0085.
Values may be sent and summed in bfloat16 or wider, within the bound.
A program may use at most 64 MiB of HBM per device.

v0:
```python
import jax
import jax.numpy as jnp
from jax import lax
from jax.sharding import PartitionSpec as P

GROUPS = 32
NEWTON = 5


EPS = 1e-05


def with_halo(block, sides, width):
    for axis, dim in sides:
        count = lax.axis_size(axis)
        forward = [(i, i + 1) for i in range(count - 1)]
        backward = [(target, source) for source, target in forward]
        low = lax.ppermute(
            lax.slice_in_dim(block, block.shape[dim] - width, None, axis=dim), axis, forward
        )
        high = lax.ppermute(lax.slice_in_dim(block, 0, width, axis=dim), axis, backward)
        block = jnp.concatenate([low, block, high], axis=dim)
    return block


def group_conv(padded, kernel):
    chans, prow, pcol = padded.shape
    height = prow - 2
    width = pcol - 2
    gwidth = chans // GROUPS
    pieces = padded.reshape(GROUPS, gwidth, prow, pcol)
    weights = kernel.reshape(GROUPS, gwidth, gwidth, 9)
    total = jnp.zeros((GROUPS, gwidth, height, width), jnp.float32)
    for position in range(9):
        shift_row, shift_col = divmod(position, 3)
        window = pieces[:, :, shift_row : shift_row + height, shift_col : shift_col + width]
        total = total + jnp.einsum(
            "goi,girw->gorw", weights[..., position], window, preferred_element_type=jnp.float32
        )
    return total.reshape(chans, height, width)


def conv_transpose(grad_pad, kernel):
    chans, prow, pcol = grad_pad.shape
    height = prow - 2
    width = pcol - 2
    gwidth = chans // GROUPS
    pieces = grad_pad.reshape(GROUPS, gwidth, prow, pcol)
    weights = kernel.reshape(GROUPS, gwidth, gwidth, 9)
    total = jnp.zeros((GROUPS, gwidth, height, width), jnp.float32)
    for position in range(9):
        shift_row, shift_col = divmod(position, 3)
        window = pieces[
            :, :, 2 - shift_row : 2 - shift_row + height, 2 - shift_col : 2 - shift_col + width
        ]
        total = total + jnp.einsum(
            "goi,gorw->girw", weights[..., position], window, preferred_element_type=jnp.float32
        )
    return total.reshape(chans, height, width)


def kernel_grad(grad_conv, padded):
    chans, height, width = grad_conv.shape
    gwidth = chans // GROUPS
    grads = grad_conv.reshape(GROUPS, gwidth, height, width)
    pieces = padded.reshape(GROUPS, gwidth, height + 2, width + 2)
    parts = []
    for position in range(9):
        shift_row, shift_col = divmod(position, 3)
        window = pieces[:, :, shift_row : shift_row + height, shift_col : shift_col + width]
        parts.append(
            jnp.einsum("gorw,girw->goi", grads, window, preferred_element_type=jnp.float32)
        )
    return jnp.stack(parts, axis=-1).reshape(chans, gwidth * 9)


def whitening(covariance):
    trace_value = jnp.trace(covariance)
    normed = covariance / trace_value
    proj = jnp.eye(covariance.shape[0], dtype=jnp.float32)
    for step in range(NEWTON):
        cube = jnp.dot(
            jnp.dot(proj, proj, precision=lax.Precision.HIGHEST),
            proj,
            precision=lax.Precision.HIGHEST,
        )
        proj = 0.5 * (3.0 * proj - jnp.dot(cube, normed, precision=lax.Precision.HIGHEST))
    return proj / jnp.sqrt(trace_value)


def local(features, group_kernel, norm_gain, norm_bias, mix_weight, cotangent):
    image = features[0]
    chans, height, width = image.shape
    local_cells = height * width
    cells = height * lax.axis_size("row") * width * lax.axis_size("col")
    scenes = features.shape[0] * lax.axis_size("dp")
    eye_mat = jnp.eye(chans, dtype=jnp.float32)
    padded = with_halo(image, (("row", 1), ("col", 2)), 1)
    conv = group_conv(padded, group_kernel).astype(jnp.bfloat16)
    flat = conv.reshape(chans, local_cells)
    channel_mean = lax.psum(jnp.sum(flat, axis=1, dtype=jnp.float32), ("row", "col")) / cells
    centered = flat.astype(jnp.float32) - channel_mean[:, None]
    moments = jnp.dot(centered, centered.T, precision=lax.Precision.HIGHEST)
    covariance = lax.psum(moments, ("row", "col")) / cells + EPS * eye_mat
    whiten = whitening(covariance)
    normed = jnp.dot(whiten, centered, precision=lax.Precision.HIGHEST)
    shifted = norm_gain[:, None] * normed + norm_bias[:, None]
    gate = jax.nn.sigmoid(shifted)
    act = (shifted * gate).astype(jnp.bfloat16)
    mixed = (
        image.reshape(chans, local_cells).astype(jnp.float32)
        + jnp.dot(mix_weight, act, preferred_element_type=jnp.float32)
    ).astype(jnp.bfloat16)
    upstream = cotangent[0].reshape(chans, local_cells)
    dact = jnp.dot(mix_weight.T, upstream, preferred_element_type=jnp.float32)
    dshift = dact * gate * (1.0 + shifted * (1.0 - gate))
    mix_part = jnp.dot(upstream, act.T, preferred_element_type=jnp.float32)
    gain_part = jnp.sum(dshift * normed, axis=1)
    bias_part = jnp.sum(dshift, axis=1)
    dnormed = (norm_gain[:, None] * dshift).astype(jnp.bfloat16)
    white_part = jnp.dot(dnormed, flat.T, preferred_element_type=jnp.float32)
    sum_part = jnp.sum(dnormed, axis=1, dtype=jnp.float32)
    white_total, grad_sum = lax.psum((white_part, sum_part), ("row", "col"))
    dwhiten = white_total - jnp.outer(grad_sum, channel_mean)
    white_out = (dwhiten / jnp.sqrt(jnp.float32(cells)))[None]
    unused, pullback = jax.vjp(whitening, covariance)
    dcov = pullback(dwhiten)[0]
    dsym = 0.5 * (dcov + dcov.T)
    left_side = jnp.concatenate([whiten.T, dsym * (2.0 / cells)], axis=1)
    right_side = jnp.concatenate(
        [dnormed.astype(jnp.float32) - (grad_sum / cells)[:, None], centered], axis=0
    )
    dconv = jnp.dot(left_side, right_side, precision=lax.Precision.HIGHEST).astype(jnp.bfloat16)
    dconv = dconv.reshape(chans, height, width)
    grad_pad = with_halo(dconv, (("row", 1), ("col", 2)), 1)
    grad_image = (cotangent[0].astype(jnp.float32) + conv_transpose(grad_pad, group_kernel)).astype(
        jnp.bfloat16
    )
    kernel_part = kernel_grad(dconv, padded)
    scale = 1.0 / jnp.sqrt(jnp.float32(scenes * cells))
    grad_mix, grad_gain, grad_bias, grad_kernel = lax.psum(
        (mix_part, gain_part, bias_part, kernel_part), ("dp", "row", "col")
    )
    return (
        mixed.reshape(features.shape),
        grad_image.reshape(features.shape),
        grad_mix * scale,
        grad_gain * scale,
        grad_bias * scale,
        grad_kernel * scale,
        white_out,
    )


def solution(mesh):
    in_specs = (P("dp", None, "row", "col"), P(), P(), P(), P(), P("dp", None, "row", "col"))
    out_specs = (
        P("dp", None, "row", "col"),
        P("dp", None, "row", "col"),
        P(),
        P(),
        P(),
        P(),
        P("dp", None, None),
    )
    return jax.shard_map(local, mesh=mesh, in_specs=in_specs, out_specs=out_specs, check_vma=False)
```

profile of v0, /device:TPU:1, one launch (start us, length us, event | category | flops | bytes accessed | tf_op | source)
XLA Modules:
  0.0 1363.5 jit_solution(14939398661312466481)
XLA Ops:
  8.4 3.9 collective-permute-start
  12.3 1.3 collective-permute-start.1
  15.0 2.3 collective-permute-done.1
  18.1 3.5 collective-permute-start.2
  22.0 1.3 collective-permute-start.3
  23.3 1.4 copy.199
  27.8 1.2 fusion.222
  32.4 296.3 %psum.56 = f32[256]{0:T(256)S(1)} all-reduce(f32[256]{0:T(256)S(1)} %reduce_sum.72), channel_id=1, replica_groups=mesh['dp'=2,'row'=16,'col'=8] {'row','col'}, use_global_device_ids=true, to_apply=%region_1.0 | all-reduce | flops 256 | bytes 2048 | tf_op jit(solution)/shard_map/psum | solution.py:101
  328.7 1.9 fusion.24
  331.4 258.6 %all-reduce.6.cloned.1.call-done = f32[256,256]{1,0:T(8,128)} async-done(((f32[256,256]{1,0:T(8,128)}), f32[256,256]{1,0:T(8,128)}) %all-reduce.6.cloned.1.call-update) | async-done | bytes 262160 | tf_op jit(solution)/shard_map/psum | solution.py:104
  599.1 1.7 fusion.217
  603.6 1.7 fusion.216
  608.2 2.9 fusion.79
  612.2 1.2 fusion.84
  613.5 2.1 fusion.220
  617.5 291.8 %psum.59 = f32[256]{0:T(256)S(1)} all-reduce(f32[256]{0:T(256)S(1)} %get-tuple-element.62), channel_id=1, replica_groups=mesh['dp'=2,'row'=16,'col'=8] {'row','col'}, use_global_device_ids=true, to_apply=%region_6.7 | all-reduce | flops 256 | bytes 2048 | tf_op jit(solution)/shard_map/psum | solution.py:123
  909.5 2.3 convolution_bitcast_fusion.1
  912.9 2.1 copy.273
  915.0 131.0 %all-reduce = (f32[256]{0:T(256)S(1)}, f32[256]{0:T(256)S(1)}) all-reduce(f32[256]{0:T(256)} %get-tuple-element.36, f32[256]{0:T(256)S(1)} %get-tuple-element.35), channel_id=1, replica_groups=mesh['dp'=2,'row'=16,'col'=8] {'dp','row','col'}, use_global_device_ids=true, to_apply=%region_11.12 | all-reduce | flops 512 | bytes 4096 | tf_op jit(solution)/shard_map/psum | solution.py:141
  1047.8 2.3 fusion.90
  1060.9 1.3 convolution_add_fusion.19
  1062.3 1.5 multiply_bitcast_fusion
  1064.4 1.6 convolution_add_fusion.18
  1069.4 1.8 multiply_reduce_fusion.1
  1072.1 2.9 fusion.8
  1079.0 3.2 collective-permute-start.4
  1082.6 1.3 collective-permute-start.5
  1084.1 3.6 collective-permute-done.5
  1088.3 3.7 collective-permute-start.6
  1092.4 1.5 collective-permute-start.7
  1095.0 2.9 copy.272
  1111.4 241.7 %all-reduce.10.cloned.1.call-done = (f32[256,256]{0,1:T(8,128)}, f32[256,72]{1,0:T(8,128)}) async-done(((f32[256,256]{0,1:T(8,128)}, f32[256,72]{1,0:T(8,128)}), (f32[256,256]{0,1:T(8,128)}, f32[256,72]{1,0:T(8,128)})) %all-reduce.10.cloned.1.call-update) | async-done | bytes 335888 | tf_op jit(solution)/shard_map/psum | solution.py:141
  (295 shorter events, 66.9 us)
Async XLA Ops:
  7.2 606.3 %copy-start = (bf16[256,256]{1,0:T(8,128)(2,1)S(1)}, bf16[256,256]{1,0:T(8,128)(2,1)}, u32[]{:S(2)}) copy-start(bf16[256,256]{1,0:T(8,128)(2,1)} %param.10) | copy-start | bytes 393220
  7.2 6.7 copy-start.76
  7.2 582.8 %all-reduce.6.cloned.1.call-start = ((), (), s32[]{:S(2)}) async-start(), calls=%async_computation | async-start | bytes 524288 | tf_op jit(solution)/shard_map/psum | solution.py:104
  8.4 6.6 collective-permute-start
  12.3 5.0 collective-permute-start.1
  15.0 578.5 %copy-start.51 = (f32[256,256]{1,0:T(8,128)}, f32[256,256]{1,0:T(8,128)S(1)}, u32[]{:S(2)}) copy-start(f32[256,256]{1,0:T(8,128)S(1)} %fusion.88) | copy-start | bytes 786436
  17.7 5.6 copy-start.20
  18.1 8.2 collective-permute-start.2
  22.0 4.7 collective-permute-start.3
  24.9 4.2 copy-start.53
  25.0 4.4 copy-start.69
  25.2 4.6 copy-start.67
  25.3 5.0 copy-start.65
  25.5 5.1 copy-start.63
  25.7 5.3 copy-start.61
  25.8 5.4 copy-start.59
  26.0 5.6 copy-start.57
  26.1 5.8 copy-start.55
  330.7 717.2 %all-reduce.8.cloned.1.call-start = ((), (), s32[]{:S(2)}) async-start(), calls=%async_computation.1 | async-start | bytes 524288 | tf_op jit(solution)/shard_map/psum | solution.py:123
  590.9 17.2 %copy-start.3 = (f32[256,256]{1,0:T(8,128)}, f32[256,256]{1,0:T(8,128)S(1)}, u32[]{:S(2)}) copy-start(f32[256,256]{1,0:T(8,128)S(1)} %multiply_add_fusion.1) | copy-start | bytes 786436
  598.7 3.2 copy-start.8
  617.4 294.3 %copy-start.2 = (f32[1,256,8,128]{1,3,2,0:T(8,128)S(1)}, f32[1,256,8,128]{1,3,2,0:T(8,128)}, u32[]{:S(2)}) copy-start(f32[1,256,8,128]{1,3,2,0:T(8,128)} %copy.199) | copy-start | bytes 3145732
  617.5 735.6 %all-reduce.10.cloned.1.call-start = ((), (), s32[]{:S(2)}) async-start(), calls=%async_computation.2 | async-start | bytes 786432 | tf_op jit(solution)/shard_map/psum | solution.py:141
  1078.2 4.1 copy-start.25
  1079.0 4.9 collective-permute-start.4
  1082.6 5.0 copy-start.41
  1082.6 5.0 collective-permute-start.5
  1087.9 6.0 copy-start.23
  1088.3 11.3 collective-permute-start.6
  1092.4 7.7 collective-permute-start.7
  1095.0 3.8 copy-start.42
  1109.7 246.9 %copy-start.1 = (bf16[256,256]{1,0:T(8,128)(2,1)S(1)}, bf16[256,256]{1,0:T(8,128)(2,1)}, u32[]{:S(2)}) copy-start(bf16[256,256]{1,0:T(8,128)(2,1)} %param.10) | copy-start | bytes 393220
  (58 other events, 90.8 us)
Sparse Core Ops, SparseCore 0:
  330.8 259.1 all-reduce.5
  617.6 213.4 all-reduce.7
  1099.8 253.2 all-reduce.9
where the time goes:
time: 1370 us; the launch traced here: 1360 us
  blocking collectives  719 us (52%)
  waiting for transfers between devices  506 us (37%)
  matrix products  55.7 us (4%)
  local copies, waits for them, and re-layouts  33.5 us (2%)
  starting transfers between devices  20.5 us (1%)
  between operations  19 us (1%)
    psum x1, blocking collectives, local(): lax.psum(jnp.sum(flat, axis=1, dtype=jnp.float32), ('row', 'col')) / cells  296 us
    psum x1, blocking collectives, local(): white_total, grad_sum = lax.psum((white_part, sum_part), ('row', 'col'))  292 us
    psum x1, waiting for transfers between devices, local(): covariance = lax.psum(moments, ('row', 'col')) / cells + EPS * eye_mat  259 us
    psum x1, waiting for transfers between devices, local(): lax.psum((mix_part, gain_part, bias_part, kernel_part), ('dp', 'row', 'co...  242 us
    psum x1, blocking collectives, local(): lax.psum((mix_part, gain_part, bias_part, kernel_part), ('dp', 'row', 'co...  131 us
  transfers between devices with their start and end apart: 11, of which 4 were waited for; matrix products, arithmetic and copies ran while one was open for 2% of the time, Pallas kernels for 0%

commit v1 on v0

v1 whole, which is shorter than its diff:
```python
import functools

import jax
import jax.numpy as jnp
from jax import lax
from jax.experimental import pallas as pl
from jax.experimental.pallas import tpu as pltpu
from jax.sharding import PartitionSpec as P

GROUPS = 32
NEWTON = 5
EPS = 1e-05
MESH = pl.DeviceIdType.MESH
F32 = jnp.float32
BF16 = jnp.bfloat16

NN = (((1,), (0,)), ((), ()))
NT = (((1,), (1,)), ((), ()))
TN = (((0,), (0,)), ((), ()))

SIDES = ((0, -1), (0, 1), (-1, -1), (-1, 1), (1, -1), (1, 1))


def mm(a, b, dims=NN):
    return lax.dot_general(a, b, dims, preferred_element_type=F32)


def split(a):
    high = a.astype(BF16)
    return high, (a - high.astype(F32)).astype(BF16)


def mm3(a, b):
    ah, al = split(a)
    bh, bl = split(b)
    return mm(jnp.concatenate([ah, ah, al], axis=1), jnp.concatenate([bh, bl, bh], axis=0))


def iota(shape, dim):
    return lax.broadcasted_iota(jnp.int32, shape, dim)


def eye_mask(n):
    return iota((n, n), 0) == iota((n, n), 1)


def to_col(row):
    n = row.shape[1]
    return jnp.sum(jnp.where(eye_mask(n), row, 0.0), axis=1, keepdims=True)


def to_row(col):
    n = col.shape[0]
    return jnp.sum(jnp.where(eye_mask(n), col, 0.0), axis=0, keepdims=True)


def kernel(
    dims,
    feat,
    kern,
    gain,
    bias,
    mix,
    cot,
    mixed_out,
    gfeat_out,
    gmix_out,
    ggain_out,
    gbias_out,
    gker_out,
    gwhite_out,
    kpad,
    kst,
    ktst,
    xpad,
    dpad,
    xedge,
    dedge,
    xrows,
    drows,
    xside,
    dside,
    conv,
    dact,
    act,
    dnorm,
    dconv,
    gacc,
    bacc,
    send1,
    recv1,
    csend1,
    crecv1,
    cov,
    send2,
    recv2,
    csend2,
    crecv2,
    white,
    send3,
    recv3,
    csend3,
    crecv3,
    gmix,
    send4,
    recv4,
    csend4,
    crecv4,
    gker,
    hsems,
    rs_s,
    rs_r,
    cx_s,
    cx_r,
    ag_s,
    ag_r,
):
    ndp, nrow, ncol, height, width = dims
    chans = feat.shape[0]
    gwidth = chans // GROUPS
    cells = height * width
    total = cells * nrow * ncol
    chunk = chans // nrow
    nwide = ndp * ncol
    block = 2 * width
    nblk = cells // block
    dp = lax.axis_index("dp")
    row = lax.axis_index("row")
    col = lax.axis_index("col")

    def row_peer(k):
        return (dp, lax.rem(row + k, nrow), col)

    def col_peer(k):
        return (dp, row, lax.rem(col + k, ncol))

    def wide_peer(k):
        slot = lax.rem(dp * ncol + col + k, nwide)
        return (slot // ncol, row, lax.rem(slot, ncol))

    def side_peer(step):
        return (
            dp,
            lax.rem(row + step[0] + nrow, nrow),
            lax.rem(col + step[1] + ncol, ncol),
        )

    barrier = pltpu.get_barrier_semaphore()

    def greet(peer):
        pl.semaphore_signal(barrier, inc=1, device_id=peer, device_id_type=MESH)

    @pl.loop(1, nrow)
    def _(k):
        greet(row_peer(k))

    @pl.loop(1, nwide)
    def _(k):
        greet(wide_peer(k))

    for step in SIDES[2:]:
        greet(side_peer(step))

    kpad[...] = jnp.zeros_like(kpad)
    kpad[:, : 9 * gwidth] = kern[...]
    own_group = (iota((chans, chans), 0) // gwidth) == (iota((chans, chans), 1) // gwidth)

    def pick(tap):
        tapcol = iota((128, chans), 0)
        within = lax.rem(iota((128, chans), 1), gwidth)
        return (tapcol == 9 * within + tap).astype(F32).astype(BF16)

    @pl.loop(0, 9)
    def _(tap):
        dense = jnp.where(own_group, mm(kpad[...], pick(tap)), 0.0)
        kst[:, pl.ds(pl.multiple_of(tap * chans, chans), chans)] = dense.astype(BF16)
        ktst[:, pl.ds(pl.multiple_of((8 - tap) * chans, chans), chans)] = dense.T.astype(BF16)

    def edges(source, edge):
        index = iota((2 * height, cells), 0)
        cell = jnp.where(index < height, index * width, (index - height) * width + width - 1)
        chosen = (iota((2 * height, cells), 1) == cell).astype(F32).astype(BF16)
        edge[...] = mm(chosen, source[...], NT).astype(BF16)

    def halo_copies(source, edge, rows, sides, base):
        copies = []
        for slot, (step, lanes) in enumerate(
            (((1, 0), pl.ds(cells - width, width)), ((-1, 0), pl.ds(0, width)))
        ):
            copies.append(
                pltpu.make_async_remote_copy(
                    src_ref=source.at[:, lanes],
                    dst_ref=rows.at[slot],
                    send_sem=hsems.at[base + slot],
                    recv_sem=hsems.at[base + 8 + slot],
                    device_id=side_peer(step),
                    device_id_type=MESH,
                )
            )
        for slot, step in enumerate(SIDES):
            copies.append(
                pltpu.make_async_remote_copy(
                    src_ref=edge,
                    dst_ref=sides.at[slot],
                    send_sem=hsems.at[base + 2 + slot],
                    recv_sem=hsems.at[base + 10 + slot],
                    device_id=side_peer((-step[0], -step[1])),
                    device_id_type=MESH,
                )
            )
        return copies

    has_up, has_down = row > 0, row < nrow - 1
    has_left, has_right = col > 0, col < ncol - 1

    def fill(source, rows, sides, pad):
        pad[1, :, width : width + cells] = source[...]
        up = jnp.where(has_up, 1.0, 0.0)
        down = jnp.where(has_down, 1.0, 0.0)
        pad[1, :, 0:width] = (rows[0].astype(F32) * up).astype(BF16)
        pad[1, :, width + cells :] = (rows[1].astype(F32) * down).astype(BF16)
        side = sides[...].reshape(8 * 2 * height, chans).astype(F32)
        live = iota((8 * 2 * height, chans), 0) < 6 * 2 * height
        side = jnp.where(live, side, 0.0).T.astype(BF16)
        tall = 2 * height

        @pl.loop(0, height + 2)
        def _(tile):
            lanes = pl.ds(pl.multiple_of(tile * width, width), width)
            value = pad[1, :, lanes].astype(F32)
            lane = iota((chans, width), 1)
            first, last = tile == 0, tile == height + 1
            vertical = jnp.logical_or(
                jnp.logical_and(first, has_up),
                jnp.logical_or(
                    jnp.logical_and(last, has_down),
                    jnp.logical_and(tile > 0, tile < height + 1),
                ),
            )
            kleft = jnp.where(
                first, 2 * tall + tall - 1, jnp.where(last, 4 * tall + height, height + tile - 1)
            )
            kright = jnp.where(
                first, 3 * tall + height - 1, jnp.where(last, 5 * tall, tall + tile - 1)
            )
            kleft = jnp.where(jnp.logical_and(vertical, has_left), kleft, -1)
            kright = jnp.where(jnp.logical_and(vertical, has_right), kright, -1)
            which = iota((8 * tall, 2 * width), 0)
            where = iota((8 * tall, 2 * width), 1)
            place = jnp.where(where == 0, kleft, jnp.where(where == 2 * width - 1, kright, -2))
            brought = mm(side, (which == place).astype(F32).astype(BF16))
            left = jnp.where(lane == 0, 0.0, pltpu.roll(value, 1, 1)) + brought[:, :width]
            right = (
                jnp.where(lane == width - 1, 0.0, pltpu.roll(value, width - 1, 1))
                + brought[:, width:]
            )
            pad[0, :, lanes] = left.astype(BF16)
            pad[2, :, lanes] = right.astype(BF16)

    def window(pad, tap, start, size):
        shift_row, shift_col = divmod(tap, 3)
        return pad[shift_col, :, pl.ds(pl.multiple_of(start + shift_row * width, width), size)]

    edges(feat, xedge)
    pl.semaphore_wait(barrier, (nrow - 1) + (nwide - 1) + 4)
    halo1 = halo_copies(feat, xedge, xrows, xside, 0)
    for copy in halo1:
        copy.start()

    @pl.loop(0, nblk)
    def _(n):
        lanes = pl.ds(pl.multiple_of(n * block, block), block)
        dact[:, lanes] = mm(mix[...], cot[:, lanes], TN)

    for copy in halo1:
        copy.wait_recv()

    fill(feat, xrows, xside, xpad)

    @pl.loop(0, nblk)
    def _(n):
        lanes = pl.ds(pl.multiple_of(n * block, block), block)
        taps = [window(xpad, tap, n * block, block) for tap in range(9)]
        conv[:, lanes] = mm(kst[...], jnp.concatenate(taps, axis=0)).astype(BF16)

    ones = jnp.ones((16, cells), BF16)

    def pack(send, full, source):
        sums = mm(ones, source[...], NT)[:8]

        for j in range(nrow):
            send[j, :chunk] = full[j * chunk : (j + 1) * chunk]
            send[j, chunk:] = sums

    def scatter(red, send, recv):
        def make(k, slot):
            return pltpu.make_async_remote_copy(
                src_ref=send.at[lax.rem(row + k, nrow)],
                dst_ref=recv.at[slot],
                send_sem=rs_s.at[red, k],
                recv_sem=rs_r.at[red, k],
                device_id=row_peer(k),
                device_id_type=MESH,
            )

        return make

    def scatter_start(red, send, recv):
        make = scatter(red, send, recv)

        @pl.loop(1, nrow)
        def _(k):
            make(k, row).start()

        recv[row] = send[row]

    def scatter_wait(red, send, recv):
        make = scatter(red, send, recv)

        @pl.loop(1, nrow)
        def _(k):
            make(k, lax.rem(row - k + nrow, nrow)).wait_recv()

        value = recv[0]
        for j in range(1, nrow):
            value = value + recv[j]
        return value

    def exchange(red, csend, crecv, wide):
        count = nwide if wide else ncol
        mine = dp * ncol + col if wide else col

        def make(k, slot):
            return pltpu.make_async_remote_copy(
                src_ref=csend,
                dst_ref=crecv.at[slot],
                send_sem=cx_s.at[red, k],
                recv_sem=cx_r.at[red, k],
                device_id=wide_peer(k) if wide else col_peer(k),
                device_id_type=MESH,
            )

        return make, count, mine

    def exchange_start(red, csend, crecv, wide, value):
        make, count, mine = exchange(red, csend, crecv, wide)
        csend[...] = value

        @pl.loop(1, count)
        def _(k):
            make(k, mine).start()

        crecv[mine] = value

    def exchange_wait(red, csend, crecv, wide):
        make, count, mine = exchange(red, csend, crecv, wide)

        @pl.loop(1, count)
        def _(k):
            make(k, lax.rem(mine - k + count, count)).wait_recv()

        value = crecv[0]
        for j in range(1, count):
            value = value + crecv[j]
        return value

    def gather(red, full):
        def make(k, owner):
            rows = pl.ds(pl.multiple_of(owner * chunk, chunk), chunk)
            return pltpu.make_async_remote_copy(
                src_ref=full.at[rows],
                dst_ref=full.at[rows],
                send_sem=ag_s.at[red, k],
                recv_sem=ag_r.at[red, k],
                device_id=row_peer(k),
                device_id_type=MESH,
            )

        return make

    def gather_start(red, full, value):
        make = gather(red, full)
        full[pl.ds(pl.multiple_of(row * chunk, chunk), chunk)] = value

        @pl.loop(1, nrow)
        def _(k):
            make(k, row).start()

    def gather_wait(red, full):
        make = gather(red, full)

        @pl.loop(1, nrow)
        def _(k):
            make(k, lax.rem(row - k + nrow, nrow)).wait_recv()

    def chunk_col(line):
        at = iota((chunk, chans), 1) == iota((chunk, chans), 0) + row * chunk
        return jnp.sum(jnp.where(at, line, 0.0), axis=1, keepdims=True)

    pack(send1, mm(conv[...], conv[...], NT), conv)
    scatter_start(0, send1, recv1)
    exchange_start(0, csend1, crecv1, False, scatter_wait(0, send1, recv1))
    moments = exchange_wait(0, csend1, crecv1, False)
    mean = moments[chunk : chunk + 1] * (1.0 / total)
    at_diag = iota((chunk, chans), 1) == iota((chunk, chans), 0) + row * chunk
    piece = moments[:chunk] * (1.0 / total) - chunk_col(mean) * mean
    gather_start(0, cov, piece + jnp.where(at_diag, EPS, 0.0))
    gather_wait(0, cov)

    diag = eye_mask(chans)
    trace = jnp.sum(
        jnp.sum(jnp.where(diag, cov[...], 0.0), axis=1, keepdims=True), axis=0, keepdims=True
    )
    inv_trace = 1.0 / trace
    inv_root = lax.rsqrt(trace)
    normal = cov[...] * inv_trace
    projs = [jnp.where(diag, 1.5, 0.0) - 0.5 * normal]
    squares, mixes = [], []
    for _ in range(1, NEWTON):
        proj = projs[-1]
        squares.append(mm3(proj, proj))
        mixes.append(mm3(proj, normal))
        projs.append(1.5 * proj - 0.5 * mm3(squares[-1], mixes[-1]))
    whiten = projs[-1] * inv_root
    wmean = jnp.sum(whiten * mean, axis=1, keepdims=True)
    whigh, wlow = split(whiten)
    wpair = jnp.concatenate([whigh, wlow], axis=1)
    gain_col = to_col(gain[...])
    bias_col = to_col(bias[...])

    gacc[...] = jnp.zeros_like(gacc)
    bacc[...] = jnp.zeros_like(bacc)

    @pl.loop(0, nblk)
    def _(n):
        lanes = pl.ds(pl.multiple_of(n * block, block), block)
        here = conv[:, lanes]
        normed = mm(wpair, jnp.concatenate([here, here], axis=0)) - wmean
        shifted = gain_col * normed + bias_col
        gate = jax.nn.sigmoid(shifted)
        act[:, lanes] = (shifted * gate).astype(BF16)
        dshift = dact[:, lanes] * gate * (1.0 + shifted * (1.0 - gate))
        dnorm[:, lanes] = (gain_col * dshift).astype(BF16)
        weighted = dshift * normed
        gacc[...] += weighted[:, :width] + weighted[:, width:]
        bacc[...] += dshift[:, :width] + dshift[:, width:]

    pack(send2, mm(dnorm[...], conv[...], NT), dnorm)
    scatter_start(1, send2, recv2)

    @pl.loop(0, nblk)
    def _(n):
        lanes = pl.ds(pl.multiple_of(n * block, block), block)
        added = feat[:, lanes].astype(F32) + mm(mix[...], act[:, lanes])
        mixed_out[:, lanes] = added.astype(BF16)

    exchange_start(1, csend2, crecv2, False, scatter_wait(1, send2, recv2))
    mix_part = mm(cot[...], act[...], NT)

    for j in range(nrow):
        send3[j] = mix_part[j * chunk : (j + 1) * chunk]

    sums2 = exchange_wait(1, csend2, crecv2, False)
    grad_sum = sums2[chunk : chunk + 1]
    gather_start(1, white, sums2[:chunk] - chunk_col(grad_sum) * mean)
    gather_wait(1, white)
    scatter_start(2, send3, recv3)

    dwhiten = white[...]
    gwhite_out[...] = dwhiten * (1.0 / float(total) ** 0.5)
    sym = 0.5 * (dwhiten + dwhiten.T)
    dproj = -0.5 * sym
    for k in range(NEWTON - 1):
        proj, square, mixp = projs[k], squares[k], mixes[k]
        dsquare = mm3(dproj, proj)
        dsquare = dsquare + dsquare.T
        dmix = mm3(dproj, normal) + mm3(proj, sym)
        dproj = 1.5 * dproj - 0.5 * (mm3(dsquare, mixp) + mm3(square, dmix))

    def full_sum(value):
        return jnp.sum(jnp.sum(value, axis=1, keepdims=True), axis=0, keepdims=True)

    scalar = full_sum(sym * projs[-1]) * 0.5 + full_sum(dproj * normal)
    dsym = inv_trace * inv_root * (dproj - jnp.where(diag, scalar, 0.0))
    dsym = (dsym + dsym.T) * (1.0 / total)
    exchange_start(2, csend3, crecv3, True, scatter_wait(2, send3, recv3))

    shift_col = (
        jnp.sum(whiten * grad_sum, axis=1, keepdims=True) * (1.0 / total)
        + jnp.sum(dsym * mean, axis=1, keepdims=True)
    )
    dhigh, dlow = split(dsym)
    quad = jnp.concatenate([whigh, wlow, dhigh, dlow], axis=1)

    @pl.loop(0, nblk)
    def _(n):
        lanes = pl.ds(pl.multiple_of(n * block, block), block)
        one, two = dnorm[:, lanes], conv[:, lanes]
        value = mm(quad, jnp.concatenate([one, one, two, two], axis=0)) - shift_col
        dconv[:, lanes] = value.astype(BF16)

    edges(dconv, dedge)
    halo2 = halo_copies(dconv, dedge, drows, dside, 16)
    for copy in halo2:
        copy.start()

    lane = iota((chans, 128), 1)
    gker_cols = jnp.where(
        lane == 9 * gwidth,
        jnp.sum(gacc[...], axis=1, keepdims=True),
        jnp.where(lane == 9 * gwidth + 1, jnp.sum(bacc[...], axis=1, keepdims=True), 0.0),
    )
    gacc[...] = gker_cols

    for tap in range(9):
        dense = mm(dconv[...], window(xpad, tap, 0, cells), NT)
        high, low = split(jnp.where(own_group, dense, 0.0))
        gacc[...] += mm(high, pick(tap), NT) + mm(low, pick(tap), NT)

    for j in range(nrow):
        send4[j] = gacc[j * chunk : (j + 1) * chunk]

    scatter_start(3, send4, recv4)
    scale = 1.0 / float(ndp * total) ** 0.5
    gather_start(2, gmix, exchange_wait(2, csend3, crecv3, True) * scale)

    for copy in halo2:
        copy.wait_recv()
    exchange_start(3, csend4, crecv4, True, scatter_wait(3, send4, recv4))
    fill(dconv, drows, dside, dpad)
    gather_start(3, gker, exchange_wait(3, csend4, crecv4, True) * scale)

    @pl.loop(0, nblk)
    def _(n):
        lanes = pl.ds(pl.multiple_of(n * block, block), block)
        taps = [window(dpad, tap, n * block, block) for tap in range(9)]
        value = mm(ktst[...], jnp.concatenate(taps, axis=0))
        gfeat_out[:, lanes] = (cot[:, lanes].astype(F32) + value).astype(BF16)

    gather_wait(2, gmix)
    gmix_out[...] = gmix[...]
    gather_wait(3, gker)
    final = gker[...]
    gker_out[...] = final[:, : 9 * gwidth]
    ggain_out[...] = to_row(final[:, 9 * gwidth : 9 * gwidth + 1])
    gbias_out[...] = to_row(final[:, 9 * gwidth + 1 : 9 * gwidth + 2])

    for copy in halo1 + halo2:
        copy.wait_send()
    for red, (send, recv, csend, crecv, full) in enumerate(
        (
            (send1, recv1, csend1, crecv1, cov),
            (send2, recv2, csend2, crecv2, white),
            (send3, recv3, csend3, crecv3, gmix),
            (send4, recv4, csend4, crecv4, gker),
        )
    ):
        one, three = scatter(red, send, recv), gather(red, full)
        two, count, mine = exchange(red, csend, crecv, red > 1)

        @pl.loop(1, nrow)
        def _(k):
            one(k, row).wait_send()
            three(k, row).wait_send()

        @pl.loop(1, count)
        def _(k):
            two(k, mine).wait_send()


def solution(mesh):
    ndp, nrow, ncol = (mesh.shape[name] for name in ("dp", "row", "col"))

    def local(features, group_kernel, norm_gain, norm_bias, mix_weight, cotangent):
        chans, height, width = features.shape[1:]
        cells = height * width
        chunk = chans // nrow
        nwide = ndp * ncol
        padded = cells + 2 * width

        def reduction(rows, cols, wide):
            return [
                pltpu.VMEM((nrow, rows, cols), F32),
                pltpu.VMEM((nrow, rows, cols), F32),
                pltpu.VMEM((rows, cols), F32),
                pltpu.VMEM((nwide if wide else ncol, rows, cols), F32),
                pltpu.VMEM((chans, cols), F32),
            ]

        vmem = pl.BlockSpec(memory_space=pltpu.VMEM)
        outs = pl.pallas_call(
            functools.partial(kernel, (ndp, nrow, ncol, height, width)),
            out_shape=(
                jax.ShapeDtypeStruct((chans, cells), BF16),
                jax.ShapeDtypeStruct((chans, cells), BF16),
                jax.ShapeDtypeStruct((chans, chans), F32),
                jax.ShapeDtypeStruct((1, chans), F32),
                jax.ShapeDtypeStruct((1, chans), F32),
                jax.ShapeDtypeStruct(group_kernel.shape, F32),
                jax.ShapeDtypeStruct((chans, chans), F32),
            ),
            in_specs=[vmem] * 6,
            out_specs=[vmem] * 7,
            scratch_shapes=[
                pltpu.VMEM((chans, 128), BF16),
                pltpu.VMEM((chans, 9 * chans), BF16),
                pltpu.VMEM((chans, 9 * chans), BF16),
                pltpu.VMEM((3, chans, padded), BF16),
                pltpu.VMEM((3, chans, padded), BF16),
                pltpu.VMEM((2 * height, chans), BF16),
                pltpu.VMEM((2 * height, chans), BF16),
                pltpu.VMEM((2, chans, width), BF16),
                pltpu.VMEM((2, chans, width), BF16),
                pltpu.VMEM((8, 2 * height, chans), BF16),
                pltpu.VMEM((8, 2 * height, chans), BF16),
                pltpu.VMEM((chans, cells), BF16),
                pltpu.VMEM((chans, cells), F32),
                pltpu.VMEM((chans, cells), BF16),
                pltpu.VMEM((chans, cells), BF16),
                pltpu.VMEM((chans, cells), BF16),
                pltpu.VMEM((chans, 128), F32),
                pltpu.VMEM((chans, 128), F32),
                *reduction(chunk + 8, chans, False),
                *reduction(chunk + 8, chans, False),
                *reduction(chunk, chans, True),
                *reduction(chunk, 128, True),
                pltpu.SemaphoreType.DMA((32,)),
                pltpu.SemaphoreType.DMA((4, nrow)),
                pltpu.SemaphoreType.DMA((4, nrow)),
                pltpu.SemaphoreType.DMA((4, nwide)),
                pltpu.SemaphoreType.DMA((4, nwide)),
                pltpu.SemaphoreType.DMA((4, nrow)),
                pltpu.SemaphoreType.DMA((4, nrow)),
            ],
            compiler_params=pltpu.CompilerParams(
                collective_id=0, has_side_effects=True, vmem_limit_bytes=60 * 1024 * 1024
            ),
        )(
            features.reshape(chans, cells),
            group_kernel,
            norm_gain.reshape(1, chans),
            norm_bias.reshape(1, chans),
            mix_weight,
            cotangent.reshape(chans, cells),
        )
        mixed, gfeat, gmix, ggain, gbias, gker, gwhite = outs
        return (
            mixed.reshape(features.shape),
            gfeat.reshape(features.shape),
            gmix,
            ggain.reshape(chans),
            gbias.reshape(chans),
            gker,
            gwhite[None],
        )

    in_specs = (P("dp", None, "row", "col"), P(), P(), P(), P(), P("dp", None, "row", "col"))
    out_specs = (
        P("dp", None, "row", "col"),
        P("dp", None, "row", "col"),
        P(),
        P(),
        P(),
        P(),
        P("dp", None, None),
    )
    return jax.shard_map(local, mesh=mesh, in_specs=in_specs, out_specs=out_specs, check_vma=False)
```

time: 1370 us -> 105 us (0.08)
  blocking collectives: 719 us -> 0 us
  waiting for transfers between devices: 506 us -> 0 us
  Pallas kernels: 0 us -> 93.9 us
  matrix products: 55.7 us -> 0 us
  local copies, waits for them, and re-layouts: 33.5 us -> 10.1 us
  starting transfers between devices: 20.5 us -> 0 us
  between operations: 19 us -> 0.66 us
    psum x3 -> x0, blocking collectives: 719 us -> none  [the longest x1 296 us: local(): lax.psum(jnp.sum(flat, axis=1, dtype=jnp.float32), ('row', 'col')) / cells]
    psum x3 -> x0, waiting for transfers between devices: 500 us -> none  [the longest x1 259 us: local(): covariance = lax.psum(moments, ('row', 'col')) / cells + EPS * eye_mat]
    pallas_call x0 -> x1, Pallas kernels: none -> 93.9 us  [local(): pl.pallas_call(functools.partial(kernel, (ndp, nrow, ncol, height, width)...]
    dot_general x74 -> x0, matrix products: 55.7 us -> none  [the longest x14 18.4 us: whitening(): jnp.dot(cube, normed, precision=lax.Precision.HIGHEST)]
    ppermute x8 -> x0, starting transfers between devices: 19.8 us -> none  [the longest x4 14.4 us: with_halo(): lax.ppermute(lax.slice_in_dim(block, block.shape[dim] - width, None, axis...]
  transfers between devices with their start and end apart: 11 -> 0, of which waited for: 4 -> 0; matrix products, arithmetic and copies ran while one was open for 2% -> 0% of each run, Pallas kernels for 0% -> 0%
where the time goes in v1:
time: 105 us
  Pallas kernels  93.9 us (89%)
  local copies, waits for them, and re-layouts  10.1 us (10%)
    pallas_call x1, Pallas kernels, local(): pl.pallas_call(functools.partial(kernel, (ndp, nrow, ncol, height, width)...  93.9 us
    unnamed x20, local copies, waits for them, and re-layouts  7.77 us
    reshape x1, local copies, waits for them, and re-layouts, local(): cotangent.reshape(chans, cells)  2.38 us

profile of v1, /device:TPU:1, one launch (start us, length us, event | category | flops | bytes accessed | tf_op | source)
XLA Modules:
  0.0 104.7 jit_solution(10510275550360217404)
XLA Ops:
  0.6 1.5 %copy.13.kern = bf16[256,72]{1,0:T(8,128)(2,1)} copy(bf16[256,72]{0,1:T(8,128)(2,1)} %param.7) | data formatting | bytes 73728 | tf_op args[1]
  2.1 2.4 %copy_bitcast_fusion = (bf16[256,1024]{1,0:T(8,128)(2,1)}, bf16[256,1024]{1,0:T(8,128)(2,1)}) fusion(bf16[32,8,8,128]{3,2,1,0:T(8,128)(2,1)} %bitcast.23, bf16[32,8,8,128]{3,2,1,0:T(8,128)(2,1)} %bitcast.24), kind=kLoop, calls=%fused_computation | loop fusion | bytes 2097152 | tf_op jit(solution)/shard_map/reshape | solution.py:644
  4.5 93.9 %shard_map.117 = (bf16[256,1024]{1,0:T(8,128)(2,1)}, bf16[256,1024]{1,0:T(8,128)(2,1)}, f32[256,256]{1,0:T(8,128)}, f32[1,256]{1,0:T(1,128)}, f32[1,256]{1,0:T(1...) custom-call(bf16[256,1024]{1,0:T(8,128)(2,1)} %get-tuple-element.29.feat, bf16[256,72]{1,0:T(8,128)(2,1)} %copy.13.kern, ...), custom_call_target="tpu_custom_call" | custom-call | tf_op jit(solution)/shard_map/pallas_call | solution.py:591
  98.4 0.0 copy-start
  98.4 2.0 %copy.17 = bf16[32,8,8,128]{3,2,1,0:T(8,128)(2,1)} copy(bf16[32,8,8,128]{3,1,2,0:T(8,128)(2,1)} %bitcast.22) | data formatting | bytes 1048576
  100.4 0.0 copy-done
  100.4 0.0 copy-start.3
  100.4 0.0 copy-start.2
  100.4 0.9 copy.18
  101.3 0.0 copy-done.3
  101.3 0.7 copy.14
  102.0 0.0 copy-done.2
  102.0 0.0 copy-start.5
  102.0 0.0 copy-start.1
  102.0 0.7 copy.25
  102.7 0.0 copy-done.5
  102.7 0.0 copy-start.4
  102.7 0.6 copy.26
  103.3 0.1 copy-done.4
  103.4 0.6 copy.27
  104.0 0.0 copy-done.1
  104.0 0.7 copy.28
Async XLA Ops:
  98.4 2.0 %copy-start = (bf16[256,1024]{1,0:T(8,128)(2,1)S(1)}, bf16[256,1024]{1,0:T(8,128)(2,1)}, u32[]{:S(2)}) copy-start(bf16[256,1024]{1,0:T(8,128)(2,1)} %get-tuple-element.15) | copy-start | bytes 1572868
  100.4 0.9 copy-start.3
  100.4 1.6 %copy-start.2 = (f32[256,256]{1,0:T(8,128)S(1)}, f32[256,256]{1,0:T(8,128)}, u32[]{:S(2)}) copy-start(f32[256,256]{1,0:T(8,128)} %get-tuple-element.39) | copy-start | bytes 786436
  102.0 0.7 copy-start.5
  102.0 1.9 %copy-start.1 = (f32[256,256]{1,0:T(8,128)S(1)}, f32[256,256]{1,0:T(8,128)}, u32[]{:S(2)}) copy-start(f32[256,256]{1,0:T(8,128)} %get-tuple-element.20) | copy-start | bytes 786436
  102.7 0.7 copy-start.4

commit v2 on v1

v2 whole, which is shorter than its diff:
```python
import functools
import math

import jax
import jax.numpy as jnp
from jax import lax
from jax.experimental import pallas as pl
from jax.experimental.pallas import tpu as pltpu
from jax.sharding import PartitionSpec as P

GROUPS = 32
NEWTON = 5
EPS = 1e-05
MESH = pl.DeviceIdType.MESH
F32 = jnp.float32
BF16 = jnp.bfloat16

NN = (((1,), (0,)), ((), ()))
NT = (((1,), (1,)), ((), ()))
TN = (((0,), (0,)), ((), ()))

SIDES = ((0, -1), (0, 1), (-1, -1), (-1, 1), (1, -1), (1, 1))


def mm(a, b, dims=NN):
    return lax.dot_general(a, b, dims, preferred_element_type=F32)


def split(a):
    high = a.astype(BF16)
    return high, (a - high.astype(F32)).astype(BF16)


def mm3(a, b):
    ah, al = split(a)
    bh, bl = split(b)
    return mm(jnp.concatenate([ah, ah, al], axis=1), jnp.concatenate([bh, bl, bh], axis=0))


def iota(shape, dim):
    return lax.broadcasted_iota(jnp.int32, shape, dim)


def eye_mask(n):
    return iota((n, n), 0) == iota((n, n), 1)


def to_col(row):
    n = row.shape[1]
    return jnp.sum(jnp.where(eye_mask(n), row, 0.0), axis=1, keepdims=True)


def gram(rows):
    high, low = split(rows)
    left = jnp.concatenate([high, high, low], axis=0)
    return mm(left, jnp.concatenate([high, low, high], axis=0), TN)


def full_sum(value):
    return jnp.sum(jnp.sum(value, axis=1, keepdims=True), axis=0, keepdims=True)


def kernel(
    dims,
    feat_in,
    kern,
    gain,
    bias,
    mix_in,
    cot_in,
    mixed_out,
    gfeat_out,
    gmix_out,
    ggain_out,
    gbias_out,
    gker_out,
    gwhite_out,
    feat,
    mix,
    cot,
    tall,
    kpad,
    kst,
    ktst,
    xpad,
    dpad,
    cot2,
    xedge,
    dedge,
    xrows,
    drows,
    xside,
    dside,
    conv,
    dact,
    act,
    dnorm,
    gacc,
    bacc,
    kgrad,
    order,
    between,
    mrow,
    msend,
    mrecv,
    mcsend,
    mcrecv,
    send1,
    recv1,
    csend1,
    crecv1,
    cov,
    send2,
    recv2,
    csend2,
    crecv2,
    white,
    send3,
    recv3,
    csend3,
    crecv3,
    gmix,
    send4,
    recv4,
    csend4,
    crecv4,
    gker,
    in_sems,
    hsems,
    rs_s,
    rs_r,
    cx_s,
    cx_r,
    ag_s,
    ag_r,
    mr_s,
    mr_r,
    mc_s,
    mc_r,
):
    ndp, nrow, ncol, height, width = dims
    chans = feat_in.shape[0]
    gwidth = chans // GROUPS
    cells = height * width
    total = cells * nrow * ncol
    chunk = chans // nrow
    nwide = ndp * ncol
    block = 2 * width
    nblk = cells // block
    edge_rows = 2 * height
    middle = slice(width, width + cells)
    dp = lax.axis_index("dp")
    row = lax.axis_index("row")
    col = lax.axis_index("col")

    side = math.isqrt(nrow)
    ys = [lax.rem(row // side + step, side) for step in range(side)]
    xs = [lax.rem(lax.rem(row, side) + step, side) for step in range(side)]
    cs = [lax.rem(col + step, ncol) for step in range(ncol)]
    dps = [lax.rem(dp + step, ndp) for step in range(ndp)]

    def far(*offsets):
        return -sum(min(step, count - step) for step, count in offsets)

    row_order = sorted(
        ((y, x) for y in range(side) for x in range(side) if y + x > 0),
        key=lambda at: far((at[0], side), (at[1], side)),
    )
    wide_order = sorted(
        ((d, c) for d in range(ndp) for c in range(ncol) if d + c > 0),
        key=lambda at: far((at[1], ncol)),
    )
    col_order = [at for at in wide_order if at[0] == 0]
    row_to = [ys[y] * side + xs[x] for y, x in row_order]
    row_from = [ys[-y % side] * side + xs[-x % side] for y, x in row_order]

    def row_peer(k):
        return (dp, row_to[k], col)

    def col_peer(k):
        return (dp, row, cs[col_order[k][1]])

    def col_from(k):
        return cs[-col_order[k][1] % ncol]

    def wide_peer(k):
        return (dps[wide_order[k][0]], row, cs[wide_order[k][1]])

    def wide_from(k):
        return dps[-wide_order[k][0] % ndp] * ncol + cs[-wide_order[k][1] % ncol]

    def side_peer(step):
        return (
            dp,
            lax.rem(row + step[0] + nrow, nrow),
            lax.rem(col + step[1] + ncol, ncol),
        )

    loads = [
        pltpu.make_async_copy(source, target, in_sems.at[i])
        for i, (source, target) in enumerate(((feat_in, feat), (mix_in, mix), (cot_in, cot)))
    ]
    for load in loads:
        load.start()
    barrier = pltpu.get_barrier_semaphore()

    def greet(peer):
        pl.semaphore_signal(barrier, inc=1, device_id=peer, device_id_type=MESH)

    for k in range(nrow - 1):
        greet(row_peer(k))
    for k in range(nwide - 1):
        greet(wide_peer(k))

    for step in SIDES[2:]:
        greet(side_peer(step))

    lane = iota((chans, width), 1)

    def put(pad, tile, value):
        lanes = pl.ds(pl.multiple_of(tile * width, width), width)
        pad[1, :, lanes] = value.astype(BF16)
        pad[0, :, lanes] = jnp.where(lane == 0, 0.0, pltpu.roll(value, 1, 1)).astype(BF16)
        pad[2, :, lanes] = jnp.where(
            lane == width - 1, 0.0, pltpu.roll(value, width - 1, 1)
        ).astype(BF16)

    def edges(source, edge):
        index = iota((edge_rows, cells), 0)
        cell = jnp.where(index < height, index * width, (index - height) * width + width - 1)
        chosen = (iota((edge_rows, cells), 1) == cell).astype(F32).astype(BF16)
        edge[...] = mm(chosen, source[1, :, middle], NT).astype(BF16)

    def halo_copies(source, edge, rows, sides, base):
        copies = []
        for slot, (step, lanes) in enumerate(
            (((1, 0), pl.ds(cells, width)), ((-1, 0), pl.ds(width, width)))
        ):
            copies.append(
                pltpu.make_async_remote_copy(
                    src_ref=source.at[1, :, lanes],
                    dst_ref=rows.at[slot],
                    send_sem=hsems.at[base + slot],
                    recv_sem=hsems.at[base + 8 + slot],
                    device_id=side_peer(step),
                    device_id_type=MESH,
                )
            )
        for slot, step in enumerate(SIDES):
            copies.append(
                pltpu.make_async_remote_copy(
                    src_ref=edge,
                    dst_ref=sides.at[slot],
                    send_sem=hsems.at[base + 2 + slot],
                    recv_sem=hsems.at[base + 10 + slot],
                    device_id=side_peer((-step[0], -step[1])),
                    device_id_type=MESH,
                )
            )
        return copies

    has_up, has_down = row > 0, row < nrow - 1
    has_left, has_right = col > 0, col < ncol - 1

    def patch(rows, sides, pad):
        side = sides[...].astype(F32).reshape(8 * edge_rows, chans).T
        at = iota((chans, 8 * edge_rows), 1) // edge_rows
        for slot, step in enumerate(SIDES):
            live = has_left if step[1] < 0 else has_right
            if step[0] < 0:
                live = jnp.logical_and(live, has_up)
            if step[0] > 0:
                live = jnp.logical_and(live, has_down)
            side = jnp.where(at == jnp.where(live, -1, slot), 0.0, side)

        def bring(slot, line, left):
            index = slot * edge_rows + line + (height if left else 0)
            shift = (0 if left else width - 1) - index
            return pltpu.roll(side, shift % (8 * edge_rows), 1)[:, :width]

        for tile, which, left, right, line, live in (
            (0, 0, 2, 3, height - 1, has_up),
            (height + 1, 1, 4, 5, 0, has_down),
        ):
            value = rows[which].astype(F32)
            value = jnp.where(live, value, 0.0)
            lanes = slice(tile * width, (tile + 1) * width)
            pad[1, :, lanes] = value.astype(BF16)
            pad[0, :, lanes] = jnp.where(
                lane == 0, bring(left, line, True), pltpu.roll(value, 1, 1)
            ).astype(BF16)
            pad[2, :, lanes] = jnp.where(
                lane == width - 1, bring(right, line, False), pltpu.roll(value, width - 1, 1)
            ).astype(BF16)
        for line in range(height):
            lanes = slice((line + 1) * width, (line + 2) * width)
            pad[0, :, lanes] = jnp.where(
                lane == 0, bring(0, line, True), pad[0, :, lanes].astype(F32)
            ).astype(BF16)
            pad[2, :, lanes] = jnp.where(
                lane == width - 1, bring(1, line, False), pad[2, :, lanes].astype(F32)
            ).astype(BF16)

    def window(pad, tap, start, size):
        shift_row, shift_col = divmod(tap, 3)
        return pad[shift_col, :, pl.ds(pl.multiple_of(start + shift_row * width, width), size)]

    def line_of(index):
        return pl.ds(index, chans, stride=height)

    loads[0].wait()
    tall[...] = feat[...].astype(F32).reshape(chans * height, width)
    for r in range(height):
        put(xpad, r + 1, tall[line_of(r), :])
    edges(xpad, xedge)
    pl.semaphore_wait(barrier, (nrow - 1) + (nwide - 1) + 4)
    halo1 = halo_copies(xpad, xedge, xrows, xside, 0)
    for copy in halo1:
        copy.start()

    kpad[...] = jnp.zeros_like(kpad)
    kpad[: 9 * gwidth] = kern[...]
    own_group = (iota((chans, chans), 0) // gwidth) == (iota((chans, chans), 1) // gwidth)

    def pick(tap):
        tapcol = iota((128, chans), 0)
        within = lax.rem(iota((128, chans), 1), gwidth)
        return (tapcol == 9 * within + tap).astype(F32).astype(BF16)

    @pl.loop(0, 9)
    def _(tap):
        dense = jnp.where(own_group, mm(kpad[...], pick(tap), TN), 0.0)
        kst[:, pl.ds(pl.multiple_of(tap * chans, chans), chans)] = dense.astype(BF16)
        other = jnp.where(own_group, mm(pick(tap), kpad[...], TN), 0.0)
        ktst[:, pl.ds(pl.multiple_of((8 - tap) * chans, chans), chans)] = other.astype(BF16)

    conv[chans:] = jnp.ones((128, cells), BF16)
    loads[1].wait()
    loads[2].wait()
    tall[...] = cot[...].astype(F32).reshape(chans * height, width)
    for r in range(height):
        cot2[:, r * width : (r + 1) * width] = tall[line_of(r), :].astype(BF16)

    @pl.loop(0, nblk)
    def _(n):
        lanes = pl.ds(pl.multiple_of(n * block, block), block)
        dact[:, lanes] = mm(mix[...], cot2[:, lanes], TN)

    for copy in halo1:
        copy.wait_recv()

    patch(xrows, xside, xpad)

    @pl.loop(0, nblk)
    def _(n):
        lanes = pl.ds(pl.multiple_of(n * block, block), block)
        taps = [window(xpad, tap, n * block, block) for tap in range(9)]
        conv[:chans, lanes] = mm(kst[...], jnp.concatenate(taps, axis=0)).astype(BF16)

    def scatter(red, send, recv, k):
        return pltpu.make_async_remote_copy(
            src_ref=send.at[row_to[k]],
            dst_ref=recv.at[k],
            send_sem=rs_s.at[red, k],
            recv_sem=rs_r.at[red, k],
            device_id=row_peer(k),
            device_id_type=MESH,
        )

    def scatter_send(red, send, recv):
        for k in range(nrow - 1):
            scatter(red, send, recv, k).start()
        recv[nrow - 1] = send[row]

    def scatter_start(red, send, recv, full):
        send[...] = full.astype(BF16).reshape(send.shape)
        scatter_send(red, send, recv)

    def ordered_sum(slots):
        value = slots[0].astype(F32)
        for j in range(1, slots.shape[0]):
            value = value + slots[j].astype(F32)
        return value

    def scatter_wait(red, send, recv):
        for k in range(nrow - 1):
            scatter(red, send, recv, k).wait_recv()
        return ordered_sum(recv)

    def exchange(red, csend, crecv, wide, k, slot):
        return pltpu.make_async_remote_copy(
            src_ref=csend,
            dst_ref=crecv.at[slot],
            send_sem=cx_s.at[red, k],
            recv_sem=cx_r.at[red, k],
            device_id=wide_peer(k) if wide else col_peer(k),
            device_id_type=MESH,
        )

    def exchange_start(red, csend, crecv, wide, value):
        mine = dp * ncol + col if wide else col
        csend[...] = value.astype(BF16)
        for k in range(crecv.shape[0] - 1):
            exchange(red, csend, crecv, wide, k, mine).start()
        crecv[mine] = value.astype(BF16)

    def exchange_wait(red, csend, crecv, wide):
        for k in range(crecv.shape[0] - 1):
            source = wide_from(k) if wide else col_from(k)
            exchange(red, csend, crecv, wide, k, source).wait_recv()
        return ordered_sum(crecv)

    def gather(red, full, k, owner):
        rows = pl.ds(pl.multiple_of(owner * chunk, chunk), chunk)
        return pltpu.make_async_remote_copy(
            src_ref=full.at[rows],
            dst_ref=full.at[rows],
            send_sem=ag_s.at[red, k],
            recv_sem=ag_r.at[red, k],
            device_id=row_peer(k),
            device_id_type=MESH,
        )

    def gather_start(red, full, value):
        full[pl.ds(pl.multiple_of(row * chunk, chunk), chunk)] = value.astype(BF16)
        for k in range(nrow - 1):
            gather(red, full, k, row).start()

    def gather_wait(red, full):
        for k in range(nrow - 1):
            gather(red, full, k, row_from[k]).wait_recv()

    def spread(red, over_row, k, slot):
        return pltpu.make_async_remote_copy(
            src_ref=(msend if over_row else mcsend).at[red],
            dst_ref=(mrecv if over_row else mcrecv).at[red, slot],
            send_sem=(mr_s if over_row else mc_s).at[red, k],
            recv_sem=(mr_r if over_row else mc_r).at[red, k],
            device_id=row_peer(k) if over_row else col_peer(k),
            device_id_type=MESH,
        )

    def spread_start(red, over_row, value):
        mine = row if over_row else col
        (msend if over_row else mcsend)[red] = value
        for k in range((nrow if over_row else ncol) - 1):
            spread(red, over_row, k, mine).start()
        (mrecv if over_row else mcrecv)[red, mine] = value

    def spread_wait(red, over_row):
        count = nrow if over_row else ncol
        for k in range(count - 1):
            spread(red, over_row, k, row_from[k] if over_row else col_from(k)).wait_recv()
        for j in range(count):
            mrow[j : j + 1] = (mrecv if over_row else mcrecv)[red, j]
        return mrow[:count]

    def row_sums(source):
        return mm(jnp.ones((16, cells), BF16), source, NT)[:1]

    def centred(source, line):
        both = mm(source, conv[...], NT)
        sums = jnp.concatenate([both[:, chans:]] * (chans // 128), axis=1)
        return both[:, :chans] - sums * line

    local_mean = row_sums(conv[:chans]) * (1.0 / cells)
    spread_start(0, True, local_mean)
    scatter_start(0, send1, recv1, centred(conv[:chans], local_mean))
    plane = spread_wait(0, True)
    plane_mean = jnp.sum(plane, axis=0, keepdims=True) * (1.0 / nrow)
    spread_start(0, False, plane_mean)
    between[...] = gram(plane - plane_mean) * float(cells)
    mine = pl.ds(pl.multiple_of(row * chunk, chunk), chunk)
    partial = scatter_wait(0, send1, recv1) + between[mine]
    exchange_start(0, csend1, crecv1, False, partial)
    gather_start(0, cov, exchange_wait(0, csend1, crecv1, False))
    planes = spread_wait(0, False)
    mean = jnp.sum(planes, axis=0, keepdims=True) * (1.0 / ncol)
    diag = eye_mask(chans)
    between[...] = gram(planes - mean) * float(cells * nrow)
    gain_col = to_col(gain[...])
    bias_col = to_col(bias[...])
    gather_wait(0, cov)

    covariance = (cov[...].astype(F32) + between[...]) * (1.0 / total) + jnp.where(diag, EPS, 0.0)
    trace = full_sum(jnp.where(diag, covariance, 0.0))
    inv_trace = 1.0 / trace
    inv_root = lax.rsqrt(trace)
    normal = covariance * inv_trace
    normal2 = mm3(normal, normal)
    projs = [jnp.where(diag, 1.5, 0.0) - 0.5 * normal]
    squares = [jnp.where(diag, 2.25, 0.0) - 1.5 * normal + 0.25 * normal2]
    mixes = [1.5 * normal - 0.5 * normal2]
    for k in range(1, NEWTON):
        if k > 1:
            squares.append(mm3(projs[-1], projs[-1]))
            mixes.append(mm3(projs[-1], normal))
        projs.append(1.5 * projs[-1] - 0.5 * mm3(squares[-1], mixes[-1]))
    whiten = projs[-1] * inv_root
    wmean = jnp.sum(whiten * mean, axis=1, keepdims=True)
    whigh, wlow = split(whiten)
    wpair = jnp.concatenate([whigh, wlow], axis=1)

    gacc[...] = jnp.zeros_like(gacc)
    bacc[...] = jnp.zeros_like(bacc)

    @pl.loop(0, nblk)
    def _(n):
        lanes = pl.ds(pl.multiple_of(n * block, block), block)
        here = conv[:chans, lanes]
        normed = mm(wpair, jnp.concatenate([here, here], axis=0)) - wmean
        shifted = gain_col * normed + bias_col
        gate = jax.nn.sigmoid(shifted)
        act[:, lanes] = (shifted * gate).astype(BF16)
        dshift = dact[:, lanes] * gate * (1.0 + shifted * (1.0 - gate))
        dnorm[:, lanes] = (gain_col * dshift).astype(BF16)
        weighted = dshift * normed
        gacc[...] += weighted[:, :width] + weighted[:, width:]
        bacc[...] += dshift[:, :width] + dshift[:, width:]

    scatter_start(1, send2, recv2, centred(dnorm[...], mean))
    spread_start(1, True, row_sums(dnorm[...]))

    for n in range(nblk):
        for half in range(2):
            r = 2 * n + half
            added = mm(mix[...], act[:, r * width : (r + 1) * width])
            added = added + xpad[1, :, (r + 1) * width : (r + 2) * width].astype(F32)
            tall[line_of(r), :] = added

    spread_start(1, False, jnp.sum(spread_wait(1, True), axis=0, keepdims=True))
    exchange_start(1, csend2, crecv2, False, scatter_wait(1, send2, recv2))
    mixed_out[...] = tall[...].reshape(chans, height, width).astype(BF16)
    send3[...] = mm(cot2[...], act[...], NT).astype(BF16).reshape(send3.shape)
    grad_sum = jnp.sum(spread_wait(1, False), axis=0, keepdims=True)
    gather_start(1, white, exchange_wait(1, csend2, crecv2, False))
    wsum = jnp.sum(whiten * grad_sum, axis=1, keepdims=True) * (1.0 / total)
    gain_sum = jnp.sum(gacc[...], axis=1, keepdims=True)
    bias_sum = jnp.sum(bacc[...], axis=1, keepdims=True)
    gather_wait(1, white)
    scatter_send(2, send3, recv3)

    dwhiten = white[...].astype(F32)
    gwhite_out[...] = dwhiten * (1.0 / float(total) ** 0.5)
    sym = 0.5 * (dwhiten + dwhiten.T)
    cross = mm3(sym, normal)
    dproj = -0.5 * sym
    for k in range(NEWTON - 1):
        if k == 0:
            dsquare = -0.75 * sym + 0.25 * cross
            dmix = 1.5 * sym - 0.5 * (cross + cross.T)
        else:
            dsquare = mm3(dproj, projs[k])
            dmix = mm3(dproj, normal) + mm3(projs[k], sym)
        dsquare = dsquare + dsquare.T
        dproj = 1.5 * dproj - 0.5 * (mm3(dsquare, mixes[k]) + mm3(squares[k], dmix))

    scalar = full_sum(sym * projs[-1]) * 0.5 + full_sum(dproj * normal)
    dsym = inv_trace * inv_root * (dproj - jnp.where(diag, scalar, 0.0))
    dsym = (dsym + dsym.T) * (1.0 / total)
    exchange_start(2, csend3, crecv3, True, scatter_wait(2, send3, recv3))

    shift_col = wsum + jnp.sum(dsym * mean, axis=1, keepdims=True)
    dhigh, dlow = split(dsym)
    quad = jnp.concatenate([whigh, wlow, dhigh, dlow], axis=1)

    @pl.loop(0, nblk)
    def _(n):
        lanes = pl.ds(pl.multiple_of(n * block, block), block)
        one, two = dnorm[:, lanes], conv[:chans, lanes]
        value = mm(quad, jnp.concatenate([one, one, two, two], axis=0)) - shift_col
        put(dpad, 2 * n + 1, value[:, :width])
        put(dpad, 2 * n + 2, value[:, width:])

    edges(dpad, dedge)
    halo2 = halo_copies(dpad, dedge, drows, dside, 16)
    for copy in halo2:
        copy.start()

    turned = dpad[1, :, middle].T

    for tap in range(9):
        dense = mm(window(xpad, tap, 0, cells), turned)
        dense = jnp.where(own_group, dense, 0.0).reshape(GROUPS, gwidth, chans)
        kgrad[tap * gwidth : (tap + 1) * gwidth] = jnp.sum(dense, axis=0)

    kgrad[9 * gwidth :] = jnp.zeros((128 - 9 * gwidth, chans), F32)
    slim = iota((chans, 128), 1)
    grads = jnp.where(slim == 9 * gwidth, gain_sum, kgrad[...].T)
    grads = jnp.where(slim == 9 * gwidth + 1, bias_sum, grads)
    scatter_start(3, send4, recv4, grads)
    scale = 1.0 / float(ndp * total) ** 0.5
    for copy in halo2:
        copy.wait_recv()
    patch(drows, dside, dpad)
    exchange_start(3, csend4, crecv4, True, scatter_wait(3, send4, recv4))
    gather_start(2, gmix, exchange_wait(2, csend3, crecv3, True) * scale)

    def back(n):
        lanes = pl.ds(pl.multiple_of(n * block, block), block)
        taps = [window(dpad, tap, n * block, block) for tap in range(9)]
        value = mm(ktst[...], jnp.concatenate(taps, axis=0)) + cot2[:, lanes].astype(F32)
        tall[line_of(2 * n), :] = value[:, :width]
        tall[line_of(2 * n + 1), :] = value[:, width:]

    @pl.loop(0, nblk)
    def _(n):
        back(n)

    gather_start(3, gker, exchange_wait(3, csend4, crecv4, True) * scale)

    gfeat_out[...] = tall[...].reshape(chans, height, width).astype(BF16)
    for copy in halo1 + halo2:
        copy.wait_send()
    everything = (
        (send1, recv1, csend1, crecv1, cov),
        (send2, recv2, csend2, crecv2, white),
        (send3, recv3, csend3, crecv3, gmix),
        (send4, recv4, csend4, crecv4, gker),
    )
    for red, (send, recv, csend, crecv, full) in enumerate(everything):
        for k in range(nrow - 1):
            scatter(red, send, recv, k).wait_send()
            if red < 3:
                gather(red, full, k, row).wait_send()
        for k in range(crecv.shape[0] - 1):
            exchange(red, csend, crecv, red > 1, k, 0).wait_send()
    for red in range(2):
        for k in range(nrow - 1):
            spread(red, True, k, 0).wait_send()
        for k in range(ncol - 1):
            spread(red, False, k, 0).wait_send()

    gather_wait(2, gmix)
    gmix_out[...] = gmix[...].astype(F32)
    gather_wait(3, gker)
    final = gker[...].astype(F32).T
    for half in range(chans // 128):
        lanes = slice(half * 128, (half + 1) * 128)
        for tap in range(9):
            lines = final[tap * gwidth : (tap + 1) * gwidth, lanes]
            order[half, pl.ds(tap, gwidth, stride=9), :] = lines
        gker_out[:, lanes] = order[half]
    ggain_out[...] = final[9 * gwidth : 9 * gwidth + 1]
    gbias_out[...] = final[9 * gwidth + 1 : 9 * gwidth + 2]
    for k in range(nrow - 1):
        gather(3, gker, k, row).wait_send()


def store(*refs):
    sems = refs[-1]
    count = len(refs) // 2
    copies = [
        pltpu.make_async_copy(refs[i], refs[count + i], sems.at[i]) for i in range(count)
    ]
    for copy in copies:
        copy.start()
    for copy in copies:
        copy.wait()


def solution(mesh):
    ndp, nrow, ncol = (mesh.shape[name] for name in ("dp", "row", "col"))

    def local(features, group_kernel, norm_gain, norm_bias, mix_weight, cotangent):
        chans, height, width = features.shape[1:]
        cells = height * width
        chunk = chans // nrow
        nwide = ndp * ncol
        padded = cells + 2 * width

        def reduction(cols, wide):
            return [
                pltpu.VMEM((nrow, chunk, cols), BF16),
                pltpu.VMEM((nrow, chunk, cols), BF16),
                pltpu.VMEM((chunk, cols), BF16),
                pltpu.VMEM((nwide if wide else ncol, chunk, cols), BF16),
                pltpu.VMEM((chans, cols), BF16),
            ]

        vmem = pl.BlockSpec(memory_space=pltpu.VMEM)
        anywhere = pl.BlockSpec(memory_space=pl.ANY)
        results = (
            ((chans, height, width), BF16),
            ((chans, height, width), BF16),
            ((chans, chans), F32),
            ((1, chans), F32),
            ((1, chans), F32),
            (group_kernel.shape[::-1], F32),
            ((chans, chans), F32),
        )
        outs = pl.pallas_call(
            functools.partial(kernel, (ndp, nrow, ncol, height, width)),
            out_shape=tuple(pltpu.VMEM(shape, dtype) for shape, dtype in results),
            in_specs=[anywhere, vmem, vmem, vmem, anywhere, anywhere],
            out_specs=[vmem] * 7,
            scratch_shapes=[
                pltpu.VMEM((chans, height, width), BF16),
                pltpu.VMEM((chans, chans), BF16),
                pltpu.VMEM((chans, height, width), BF16),
                pltpu.VMEM((chans * height, width), F32),
                pltpu.VMEM((128, chans), BF16),
                pltpu.VMEM((chans, 9 * chans), BF16),
                pltpu.VMEM((chans, 9 * chans), BF16),
                pltpu.VMEM((3, chans, padded), BF16),
                pltpu.VMEM((3, chans, padded), BF16),
                pltpu.VMEM((chans, cells), BF16),
                pltpu.VMEM((2 * height, chans), BF16),
                pltpu.VMEM((2 * height, chans), BF16),
                pltpu.VMEM((2, chans, width), BF16),
                pltpu.VMEM((2, chans, width), BF16),
                pltpu.VMEM((8, 2 * height, chans), BF16),
                pltpu.VMEM((8, 2 * height, chans), BF16),
                pltpu.VMEM((chans + 128, cells), BF16),
                pltpu.VMEM((chans, cells), F32),
                pltpu.VMEM((chans, cells), BF16),
                pltpu.VMEM((chans, cells), BF16),
                pltpu.VMEM((chans, 128), F32),
                pltpu.VMEM((chans, 128), F32),
                pltpu.VMEM((128, chans), F32),
                pltpu.VMEM((chans // 128, group_kernel.shape[1], 128), F32),
                pltpu.VMEM((chans, chans), F32),
                pltpu.VMEM((max(nrow, ncol), chans), F32),
                pltpu.VMEM((2, 1, chans), F32),
                pltpu.VMEM((2, nrow, 1, chans), F32),
                pltpu.VMEM((2, 1, chans), F32),
                pltpu.VMEM((2, ncol, 1, chans), F32),
                *reduction(chans, False),
                *reduction(chans, False),
                *reduction(chans, True),
                *reduction(128, True),
                pltpu.SemaphoreType.DMA((3,)),
                pltpu.SemaphoreType.DMA((32,)),
                pltpu.SemaphoreType.DMA((4, nrow)),
                pltpu.SemaphoreType.DMA((4, nrow)),
                pltpu.SemaphoreType.DMA((4, nwide)),
                pltpu.SemaphoreType.DMA((4, nwide)),
                pltpu.SemaphoreType.DMA((4, nrow)),
                pltpu.SemaphoreType.DMA((4, nrow)),
                pltpu.SemaphoreType.DMA((2, nrow)),
                pltpu.SemaphoreType.DMA((2, nrow)),
                pltpu.SemaphoreType.DMA((2, ncol)),
                pltpu.SemaphoreType.DMA((2, ncol)),
            ],
            compiler_params=pltpu.CompilerParams(
                collective_id=0, has_side_effects=True, vmem_limit_bytes=60 * 1024 * 1024
            ),
        )(
            features.reshape(chans, height, width),
            group_kernel.T,
            norm_gain.reshape(1, chans),
            norm_bias.reshape(1, chans),
            mix_weight,
            cotangent.reshape(chans, height, width),
        )
        mixed, gfeat, gmix, ggain, gbias, gker, gwhite = pl.pallas_call(
            store,
            out_shape=tuple(jax.ShapeDtypeStruct(shape, dtype) for shape, dtype in results),
            in_specs=[anywhere] * 7,
            out_specs=[anywhere] * 7,
            scratch_shapes=[pltpu.SemaphoreType.DMA((7,))],
        )(*(pltpu.with_memory_space_constraint(out, pltpu.VMEM) for out in outs))
        return (
            mixed.reshape(features.shape),
            gfeat.reshape(features.shape),
            gmix,
            ggain.reshape(chans),
            gbias.reshape(chans),
            gker.T,
            gwhite[None],
        )

    in_specs = (P("dp", None, "row", "col"), P(), P(), P(), P(), P("dp", None, "row", "col"))
    out_specs = (
        P("dp", None, "row", "col"),
        P("dp", None, "row", "col"),
        P(),
        P(),
        P(),
        P(),
        P("dp", None, None),
    )
    return jax.shard_map(local, mesh=mesh, in_specs=in_specs, out_specs=out_specs, check_vma=False)
```

time: 105 us -> 83.4 us (0.79)
  Pallas kernels: 93.9 us -> 82.6 us
  local copies, waits for them, and re-layouts: 10.1 us -> 0 us
    pallas_call x1, Pallas kernels: 93.9 us -> 81.4 us  [local(): pl.pallas_call(functools.partial(kernel, (ndp, nrow, ncol, height, width)...]
    unnamed x20 -> x0, local copies, waits for them, and re-layouts: 7.77 us -> none
    reshape x1 -> x0, local copies, waits for them, and re-layouts: 2.38 us -> none  [local(): cotangent.reshape(chans, cells)]
    pallas_call x0 -> x1, Pallas kernels: none -> 1.23 us  [local(): pl.pallas_call(store, out_shape=tuple((jax.ShapeDtypeStruct(shape, dtype)...]
where the time goes in v2:
time: 83.4 us; the launch traced here: 83.2 us
  Pallas kernels  82.6 us (99%)
    pallas_call x1, Pallas kernels, local(): pl.pallas_call(functools.partial(kernel, (ndp, nrow, ncol, height, width)...  81.4 us

profile of v2, /device:TPU:1, one launch (start us, length us, event | category | flops | bytes accessed | tf_op | source)
XLA Modules:
  0.0 83.2 jit_solution(10912901909120803790)
XLA Ops:
  0.6 81.4 %shard_map.117 = (bf16[256,8,128]{2,1,0:T(8,128)(2,1)S(1)}, bf16[256,8,128]{2,1,0:T(8,128)(2,1)S(1)}, f32[256,256]{1,0:T(8,128)S(1)}, f32[1,256]{1,0:T(1,128)S(1...) custom-call(bf16[256,8,128]{2,1,0:T(8,128)(2,1)} %bitcast.11, bf16[72,256]{1,0:T(8,128)(2,1)} %bitcast.13, ...), custom_call_target="tpu_custom_call" | custom-call | tf_op jit(solution)/shard_map/pallas_call | solution.py:692
  82.0 1.2 %shard_map.118 = (bf16[256,8,128]{2,1,0:T(8,128)(2,1)}, bf16[256,8,128]{2,1,0:T(8,128)(2,1)}, f32[256,256]{1,0:T(8,128)}, f32[1,256]{1,0:T(1,128)}, f32[1,256]{1...) custom-call(bf16[256,8,128]{2,1,0:T(8,128)(2,1)S(1)} %get-tuple-element.21.refs_0_, ...), custom_call_target="tpu_custom_call" | custom-call | tf_op jit(solution)/shard_map/pallas_call | solution.py:756

commit v3 on v2

--- a/solution.py
+++ b/solution.py
@@ -63,9 +63,9 @@
 def kernel(
     dims,
     feat_in,
-    kern,
-    gain,
-    bias,
+    kern_in,
+    gain_in,
+    bias_in,
     mix_in,
     cot_in,
     mixed_out,
@@ -78,6 +78,9 @@
     feat,
     mix,
     cot,
+    kern,
+    gain,
+    bias,
     tall,
     kpad,
     kst,
@@ -172,7 +175,6 @@
     )
     col_order = [at for at in wide_order if at[0] == 0]
     row_to = [ys[y] * side + xs[x] for y, x in row_order]
-    row_from = [ys[-y % side] * side + xs[-x % side] for y, x in row_order]
 
     def row_peer(k):
         return (dp, row_to[k], col)
@@ -180,14 +182,8 @@
     def col_peer(k):
         return (dp, row, cs[col_order[k][1]])
 
-    def col_from(k):
-        return cs[-col_order[k][1] % ncol]
-
     def wide_peer(k):
         return (dps[wide_order[k][0]], row, cs[wide_order[k][1]])
-
-    def wide_from(k):
-        return dps[-wide_order[k][0] % ndp] * ncol + cs[-wide_order[k][1] % ncol]
 
     def side_peer(step):
         return (
@@ -196,12 +192,31 @@
             lax.rem(col + step[1] + ncol, ncol),
         )
 
+    arguments = (
+        (feat_in, feat),
+        (mix_in, mix),
+        (cot_in, cot),
+        (kern_in, kern),
+        (gain_in, gain),
+        (bias_in, bias),
+    )
     loads = [
         pltpu.make_async_copy(source, target, in_sems.at[i])
-        for i, (source, target) in enumerate(((feat_in, feat), (mix_in, mix), (cot_in, cot)))
+        for i, (source, target) in enumerate(arguments)
     ]
     for load in loads:
         load.start()
+    def whole(ref, count, send_sem, recv_sem):
+        part = ref.at[pl.ds(0, count)]
+        return pltpu.make_async_remote_copy(
+            src_ref=part,
+            dst_ref=part,
+            send_sem=send_sem,
+            recv_sem=recv_sem,
+            device_id=row_peer(0),
+            device_id_type=MESH,
+        )
+
     barrier = pltpu.get_barrier_semaphore()
 
     def greet(peer):
@@ -240,8 +255,8 @@
                 pltpu.make_async_remote_copy(
                     src_ref=source.at[1, :, lanes],
                     dst_ref=rows.at[slot],
-                    send_sem=hsems.at[base + slot],
-                    recv_sem=hsems.at[base + 8 + slot],
+                    send_sem=hsems.at[base],
+                    recv_sem=hsems.at[base + 1],
                     device_id=side_peer(step),
                     device_id_type=MESH,
                 )
@@ -251,18 +266,25 @@
                 pltpu.make_async_remote_copy(
                     src_ref=edge,
                     dst_ref=sides.at[slot],
-                    send_sem=hsems.at[base + 2 + slot],
-                    recv_sem=hsems.at[base + 10 + slot],
+                    send_sem=hsems.at[base + 2],
+                    recv_sem=hsems.at[base + 3],
                     device_id=side_peer((-step[0], -step[1])),
                     device_id_type=MESH,
                 )
             )
-        return copies
+        for copy in copies:
+            copy.start()
+
+    def halo_waits(rows, sides, base):
+        return (
+            whole(rows, 2, hsems.at[base], hsems.at[base + 1]),
+            whole(sides, len(SIDES), hsems.at[base + 2], hsems.at[base + 3]),
+        )
 
     has_up, has_down = row > 0, row < nrow - 1
     has_left, has_right = col > 0, col < ncol - 1
 
-    def patch(rows, sides, pad):
+    def patch(rows, sides, pad, fresh):
         side = sides[...].astype(F32).reshape(8 * edge_rows, chans).T
         at = iota((chans, 8 * edge_rows), 1) // edge_rows
         for slot, step in enumerate(SIDES):
@@ -294,11 +316,14 @@
             ).astype(BF16)
         for line in range(height):
             lanes = slice((line + 1) * width, (line + 2) * width)
-            pad[0, :, lanes] = jnp.where(
-                lane == 0, bring(0, line, True), pad[0, :, lanes].astype(F32)
-            ).astype(BF16)
+            if fresh:
+                value = pad[1, :, lanes].astype(F32)
+                before, after = pltpu.roll(value, 1, 1), pltpu.roll(value, width - 1, 1)
+            else:
+                before, after = pad[0, :, lanes].astype(F32), pad[2, :, lanes].astype(F32)
+            pad[0, :, lanes] = jnp.where(lane == 0, bring(0, line, True), before).astype(BF16)
             pad[2, :, lanes] = jnp.where(
-                lane == width - 1, bring(1, line, False), pad[2, :, lanes].astype(F32)
+                lane == width - 1, bring(1, line, False), after
             ).astype(BF16)
 
     def window(pad, tap, start, size):
@@ -314,10 +339,10 @@
         put(xpad, r + 1, tall[line_of(r), :])
     edges(xpad, xedge)
     pl.semaphore_wait(barrier, (nrow - 1) + (nwide - 1) + 4)
-    halo1 = halo_copies(xpad, xedge, xrows, xside, 0)
-    for copy in halo1:
-        copy.start()
-
+    halo_copies(xpad, xedge, xrows, xside, 0)
+
+    for load in loads[3:]:
+        load.wait()
     kpad[...] = jnp.zeros_like(kpad)
     kpad[: 9 * gwidth] = kern[...]
     own_group = (iota((chans, chans), 0) // gwidth) == (iota((chans, chans), 1) // gwidth)
@@ -346,10 +371,10 @@
         lanes = pl.ds(pl.multiple_of(n * block, block), block)
         dact[:, lanes] = mm(mix[...], cot2[:, lanes], TN)
 
-    for copy in halo1:
-        copy.wait_recv()
-
-    patch(xrows, xside, xpad)
+    for wait in halo_waits(xrows, xside, 0):
+        wait.wait_recv()
+
+    patch(xrows, xside, xpad, False)
 
     @pl.loop(0, nblk)
     def _(n):
@@ -357,12 +382,26 @@
         taps = [window(xpad, tap, n * block, block) for tap in range(9)]
         conv[:chans, lanes] = mm(kst[...], jnp.concatenate(taps, axis=0)).astype(BF16)
 
+    def all_scattered(red, recv):
+        return whole(recv, nrow - 1, rs_s.at[red], rs_r.at[red])
+
+    def all_exchanged(red, crecv):
+        return whole(crecv, crecv.shape[0] - 1, cx_s.at[red], cx_r.at[red])
+
+    def all_gathered(red, full):
+        return whole(full, chans - chunk, ag_s.at[red], ag_r.at[red])
+
+    def all_spread(red, over_row):
+        if over_row:
+            return whole(mrecv.at[red], nrow - 1, mr_s.at[red], mr_r.at[red])
+        return whole(mcrecv.at[red], ncol - 1, mc_s.at[red], mc_r.at[red])
+
     def scatter(red, send, recv, k):
         return pltpu.make_async_remote_copy(
             src_ref=send.at[row_to[k]],
             dst_ref=recv.at[k],
-            send_sem=rs_s.at[red, k],
-            recv_sem=rs_r.at[red, k],
+            send_sem=rs_s.at[red],
+            recv_sem=rs_r.at[red],
             device_id=row_peer(k),
             device_id_type=MESH,
         )
@@ -383,16 +422,15 @@
         return value
 
     def scatter_wait(red, send, recv):
-        for k in range(nrow - 1):
-            scatter(red, send, recv, k).wait_recv()
+        all_scattered(red, recv).wait_recv()
         return ordered_sum(recv)
 
     def exchange(red, csend, crecv, wide, k, slot):
         return pltpu.make_async_remote_copy(
             src_ref=csend,
             dst_ref=crecv.at[slot],
-            send_sem=cx_s.at[red, k],
-            recv_sem=cx_r.at[red, k],
+            send_sem=cx_s.at[red],
+            recv_sem=cx_r.at[red],
             device_id=wide_peer(k) if wide else col_peer(k),
             device_id_type=MESH,
         )
@@ -405,9 +443,7 @@
         crecv[mine] = value.astype(BF16)
 
     def exchange_wait(red, csend, crecv, wide):
-        for k in range(crecv.shape[0] - 1):
-            source = wide_from(k) if wide else col_from(k)
-            exchange(red, csend, crecv, wide, k, source).wait_recv()
+        all_exchanged(red, crecv).wait_recv()
         return ordered_sum(crecv)
 
     def gather(red, full, k, owner):
@@ -415,8 +451,8 @@
         return pltpu.make_async_remote_copy(
             src_ref=full.at[rows],
             dst_ref=full.at[rows],
-            send_sem=ag_s.at[red, k],
-            recv_sem=ag_r.at[red, k],
+            send_sem=ag_s.at[red],
+            recv_sem=ag_r.at[red],
             device_id=row_peer(k),
             device_id_type=MESH,
         )
@@ -427,15 +463,14 @@
             gather(red, full, k, row).start()
 
     def gather_wait(red, full):
-        for k in range(nrow - 1):
-            gather(red, full, k, row_from[k]).wait_recv()
+        all_gathered(red, full).wait_recv()
 
     def spread(red, over_row, k, slot):
         return pltpu.make_async_remote_copy(
             src_ref=(msend if over_row else mcsend).at[red],
             dst_ref=(mrecv if over_row else mcrecv).at[red, slot],
-            send_sem=(mr_s if over_row else mc_s).at[red, k],
-            recv_sem=(mr_r if over_row else mc_r).at[red, k],
+            send_sem=(mr_s if over_row else mc_s).at[red],
+            recv_sem=(mr_r if over_row else mc_r).at[red],
             device_id=row_peer(k) if over_row else col_peer(k),
             device_id_type=MESH,
         )
@@ -449,8 +484,7 @@
 
     def spread_wait(red, over_row):
         count = nrow if over_row else ncol
-        for k in range(count - 1):
-            spread(red, over_row, k, row_from[k] if over_row else col_from(k)).wait_recv()
+        all_spread(red, over_row).wait_recv()
         for j in range(count):
             mrow[j : j + 1] = (mrecv if over_row else mcrecv)[red, j]
         return mrow[:count]
@@ -458,14 +492,13 @@
     def row_sums(source):
         return mm(jnp.ones((16, cells), BF16), source, NT)[:1]
 
-    def centred(source, line):
-        both = mm(source, conv[...], NT)
+    def centred(both, line):
         sums = jnp.concatenate([both[:, chans:]] * (chans // 128), axis=1)
         return both[:, :chans] - sums * line
 
     local_mean = row_sums(conv[:chans]) * (1.0 / cells)
     spread_start(0, True, local_mean)
-    scatter_start(0, send1, recv1, centred(conv[:chans], local_mean))
+    scatter_start(0, send1, recv1, centred(mm(conv[:chans], conv[...], NT), local_mean))
     plane = spread_wait(0, True)
     plane_mean = jnp.sum(plane, axis=0, keepdims=True) * (1.0 / nrow)
     spread_start(0, False, plane_mean)
@@ -501,24 +534,25 @@
     whigh, wlow = split(whiten)
     wpair = jnp.concatenate([whigh, wlow], axis=1)
 
-    gacc[...] = jnp.zeros_like(gacc)
-    bacc[...] = jnp.zeros_like(bacc)
-
-    @pl.loop(0, nblk)
-    def _(n):
-        lanes = pl.ds(pl.multiple_of(n * block, block), block)
+    gain_part, bias_part, product = 0.0, 0.0, 0.0
+    for n in range(nblk):
+        lanes = slice(n * block, (n + 1) * block)
         here = conv[:chans, lanes]
         normed = mm(wpair, jnp.concatenate([here, here], axis=0)) - wmean
         shifted = gain_col * normed + bias_col
         gate = jax.nn.sigmoid(shifted)
         act[:, lanes] = (shifted * gate).astype(BF16)
         dshift = dact[:, lanes] * gate * (1.0 + shifted * (1.0 - gate))
-        dnorm[:, lanes] = (gain_col * dshift).astype(BF16)
+        grads = (gain_col * dshift).astype(BF16)
+        dnorm[:, lanes] = grads
+        product = product + mm(grads, conv[:, lanes], NT)
         weighted = dshift * normed
-        gacc[...] += weighted[:, :width] + weighted[:, width:]
-        bacc[...] += dshift[:, :width] + dshift[:, width:]
-
-    scatter_start(1, send2, recv2, centred(dnorm[...], mean))
+        gain_part = gain_part + weighted[:, :width] + weighted[:, width:]
+        bias_part = bias_part + dshift[:, :width] + dshift[:, width:]
+    gacc[...] = gain_part
+    bacc[...] = bias_part
+
+    scatter_start(1, send2, recv2, centred(product, mean))
     spread_start(1, True, row_sums(dnorm[...]))
 
     for n in range(nblk):
@@ -569,13 +603,7 @@
         lanes = pl.ds(pl.multiple_of(n * block, block), block)
         one, two = dnorm[:, lanes], conv[:chans, lanes]
         value = mm(quad, jnp.concatenate([one, one, two, two], axis=0)) - shift_col
-        put(dpad, 2 * n + 1, value[:, :width])
-        put(dpad, 2 * n + 2, value[:, width:])
-
-    edges(dpad, dedge)
-    halo2 = halo_copies(dpad, dedge, drows, dside, 16)
-    for copy in halo2:
-        copy.start()
+        dpad[1, :, pl.ds(pl.multiple_of(n * block + width, width), block)] = value.astype(BF16)
 
     turned = dpad[1, :, middle].T
 
@@ -590,11 +618,13 @@
     grads = jnp.where(slim == 9 * gwidth + 1, bias_sum, grads)
     scatter_start(3, send4, recv4, grads)
     scale = 1.0 / float(ndp * total) ** 0.5
-    for copy in halo2:
-        copy.wait_recv()
-    patch(drows, dside, dpad)
+    edges(dpad, dedge)
+    halo_copies(dpad, dedge, drows, dside, 4)
     exchange_start(3, csend4, crecv4, True, scatter_wait(3, send4, recv4))
     gather_start(2, gmix, exchange_wait(2, csend3, crecv3, True) * scale)
+    for wait in halo_waits(drows, dside, 4):
+        wait.wait_recv()
+    patch(drows, dside, dpad, True)
 
     def back(n):
         lanes = pl.ds(pl.multiple_of(n * block, block), block)
@@ -610,8 +640,8 @@
     gather_start(3, gker, exchange_wait(3, csend4, crecv4, True) * scale)
 
     gfeat_out[...] = tall[...].reshape(chans, height, width).astype(BF16)
-    for copy in halo1 + halo2:
-        copy.wait_send()
+    for wait in halo_waits(xrows, xside, 0) + halo_waits(drows, dside, 4):
+        wait.wait_send()
     everything = (
         (send1, recv1, csend1, crecv1, cov),
         (send2, recv2, csend2, crecv2, white),
@@ -619,17 +649,13 @@
         (send4, recv4, csend4, crecv4, gker),
     )
     for red, (send, recv, csend, crecv, full) in enumerate(everything):
-        for k in range(nrow - 1):
-            scatter(red, send, recv, k).wait_send()
-            if red < 3:
-                gather(red, full, k, row).wait_send()
-        for k in range(crecv.shape[0] - 1):
-            exchange(red, csend, crecv, red > 1, k, 0).wait_send()
+        all_scattered(red, recv).wait_send()
+        all_exchanged(red, crecv).wait_send()
+        if red < 3:
+            all_gathered(red, full).wait_send()
     for red in range(2):
-        for k in range(nrow - 1):
-            spread(red, True, k, 0).wait_send()
-        for k in range(ncol - 1):
-            spread(red, False, k, 0).wait_send()
+        all_spread(red, True).wait_send()
+        all_spread(red, False).wait_send()
 
     gather_wait(2, gmix)
     gmix_out[...] = gmix[...].astype(F32)
@@ -643,8 +669,7 @@
         gker_out[:, lanes] = order[half]
     ggain_out[...] = final[9 * gwidth : 9 * gwidth + 1]
     gbias_out[...] = final[9 * gwidth + 1 : 9 * gwidth + 2]
-    for k in range(nrow - 1):
-        gather(3, gker, k, row).wait_send()
+    all_gathered(3, gker).wait_send()
 
 
 def store(*refs):
@@ -692,12 +717,15 @@
         outs = pl.pallas_call(
             functools.partial(kernel, (ndp, nrow, ncol, height, width)),
             out_shape=tuple(pltpu.VMEM(shape, dtype) for shape, dtype in results),
-            in_specs=[anywhere, vmem, vmem, vmem, anywhere, anywhere],
+            in_specs=[anywhere] * 6,
             out_specs=[vmem] * 7,
             scratch_shapes=[
                 pltpu.VMEM((chans, height, width), BF16),
                 pltpu.VMEM((chans, chans), BF16),
                 pltpu.VMEM((chans, height, width), BF16),
+                pltpu.VMEM(group_kernel.shape[::-1], BF16),
+                pltpu.VMEM((1, chans), F32),
+                pltpu.VMEM((1, chans), F32),
                 pltpu.VMEM((chans * height, width), F32),
                 pltpu.VMEM((128, chans), BF16),
                 pltpu.VMEM((chans, 9 * chans), BF16),
@@ -729,18 +757,10 @@
                 *reduction(chans, False),
                 *reduction(chans, True),
                 *reduction(128, True),
-                pltpu.SemaphoreType.DMA((3,)),
-                pltpu.SemaphoreType.DMA((32,)),
-                pltpu.SemaphoreType.DMA((4, nrow)),
-                pltpu.SemaphoreType.DMA((4, nrow)),
-                pltpu.SemaphoreType.DMA((4, nwide)),
-                pltpu.SemaphoreType.DMA((4, nwide)),
-                pltpu.SemaphoreType.DMA((4, nrow)),
-                pltpu.SemaphoreType.DMA((4, nrow)),
-                pltpu.SemaphoreType.DMA((2, nrow)),
-                pltpu.SemaphoreType.DMA((2, nrow)),
-                pltpu.SemaphoreType.DMA((2, ncol)),
-                pltpu.SemaphoreType.DMA((2, ncol)),
+                pltpu.SemaphoreType.DMA((6,)),
+                pltpu.SemaphoreType.DMA((8,)),
+                *[pltpu.SemaphoreType.DMA((4,))] * 6,
+                *[pltpu.SemaphoreType.DMA((2,))] * 4,
             ],
             compiler_params=pltpu.CompilerParams(
                 collective_id=0, has_side_effects=True, vmem_limit_bytes=60 * 1024 * 1024

time: 83.4 us -> 76.5 us (0.917)
  Pallas kernels: 82.6 us -> 75.7 us
    pallas_call x1, Pallas kernels: 81.4 us -> 74.5 us  [local(): pl.pallas_call(functools.partial(kernel, (ndp, nrow, ncol, height, width)...]
where the time goes in v3:
time: 76.5 us; the launch traced here: 76.4 us
  Pallas kernels  75.7 us (99%)
    pallas_call x1, Pallas kernels, local(): pl.pallas_call(functools.partial(kernel, (ndp, nrow, ncol, height, width)...  74.5 us

profile of v3, /device:TPU:1, one launch (start us, length us, event | category | flops | bytes accessed | tf_op | source)
XLA Modules:
  0.0 76.4 jit_solution(12725218927746080315)
XLA Ops:
  0.6 74.5 %shard_map.117 = (bf16[256,8,128]{2,1,0:T(8,128)(2,1)S(1)}, bf16[256,8,128]{2,1,0:T(8,128)(2,1)S(1)}, f32[256,256]{1,0:T(8,128)S(1)}, f32[1,256]{1,0:T(1,128)S(1...) custom-call(bf16[256,8,128]{2,1,0:T(8,128)(2,1)} %bitcast.11, bf16[72,256]{1,0:T(8,128)(2,1)} %bitcast.13, ...), custom_call_target="tpu_custom_call" | custom-call | tf_op jit(solution)/shard_map/pallas_call | solution.py:717
  75.1 1.2 %shard_map.118 = (bf16[256,8,128]{2,1,0:T(8,128)(2,1)}, bf16[256,8,128]{2,1,0:T(8,128)(2,1)}, f32[256,256]{1,0:T(8,128)}, f32[1,256]{1,0:T(1,128)}, f32[1,256]{1...) custom-call(bf16[256,8,128]{2,1,0:T(8,128)(2,1)S(1)} %get-tuple-element.21.refs_0_, ...), custom_call_target="tpu_custom_call" | custom-call | tf_op jit(solution)/shard_map/pallas_call | solution.py:776

commit v4 on v3

--- a/solution.py
+++ b/solution.py
@@ -31,10 +31,14 @@
     return high, (a - high.astype(F32)).astype(BF16)
 
 
-def mm3(a, b):
-    ah, al = split(a)
-    bh, bl = split(b)
-    return mm(jnp.concatenate([ah, ah, al], axis=1), jnp.concatenate([bh, bl, bh], axis=0))
+def left(a):
+    high, low = split(a)
+    return jnp.concatenate([high, high, low], axis=1)
+
+
+def right(b):
+    high, low = split(b)
+    return jnp.concatenate([high, low, high], axis=0)
 
 
 def iota(shape, dim):
@@ -95,6 +99,7 @@
     xside,
     dside,
     conv,
+    alone,
     dact,
     act,
     dnorm,
@@ -104,6 +109,8 @@
     order,
     between,
     mrow,
+    mplane,
+    mblock,
     msend,
     mrecv,
     mcsend,
@@ -284,8 +291,8 @@
     has_up, has_down = row > 0, row < nrow - 1
     has_left, has_right = col > 0, col < ncol - 1
 
-    def patch(rows, sides, pad, fresh):
-        side = sides[...].astype(F32).reshape(8 * edge_rows, chans).T
+    def side_lanes(sides):
+        side_map = sides[...].astype(F32).reshape(8 * edge_rows, chans).T
         at = iota((chans, 8 * edge_rows), 1) // edge_rows
         for slot, step in enumerate(SIDES):
             live = has_left if step[1] < 0 else has_right
@@ -293,27 +300,32 @@
                 live = jnp.logical_and(live, has_up)
             if step[0] > 0:
                 live = jnp.logical_and(live, has_down)
-            side = jnp.where(at == jnp.where(live, -1, slot), 0.0, side)
-
-        def bring(slot, line, left):
-            index = slot * edge_rows + line + (height if left else 0)
-            shift = (0 if left else width - 1) - index
-            return pltpu.roll(side, shift % (8 * edge_rows), 1)[:, :width]
-
-        for tile, which, left, right, line, live in (
+            side_map = jnp.where(at == jnp.where(live, -1, slot), 0.0, side_map)
+        return jnp.where(at < len(SIDES), side_map, 0.0)
+
+    def bring(side_map, slot, line, first):
+        index = slot * edge_rows + line + (height if first else 0)
+        shift = (0 if first else width - 1) - index
+        return pltpu.roll(side_map, shift % (8 * edge_rows), 1)[:, :width]
+
+    def put_ends(rows, side_map, pad):
+        for tile, which, before, after, line, live in (
             (0, 0, 2, 3, height - 1, has_up),
             (height + 1, 1, 4, 5, 0, has_down),
         ):
-            value = rows[which].astype(F32)
-            value = jnp.where(live, value, 0.0)
+            value = jnp.where(live, rows[which].astype(F32), 0.0)
             lanes = slice(tile * width, (tile + 1) * width)
             pad[1, :, lanes] = value.astype(BF16)
             pad[0, :, lanes] = jnp.where(
-                lane == 0, bring(left, line, True), pltpu.roll(value, 1, 1)
+                lane == 0, bring(side_map, before, line, True), pltpu.roll(value, 1, 1)
             ).astype(BF16)
             pad[2, :, lanes] = jnp.where(
-                lane == width - 1, bring(right, line, False), pltpu.roll(value, width - 1, 1)
+                lane == width - 1,
+                bring(side_map, after, line, False),
+                pltpu.roll(value, width - 1, 1),
             ).astype(BF16)
+
+    def put_columns(side_map, pad, fresh):
         for line in range(height):
             lanes = slice((line + 1) * width, (line + 2) * width)
             if fresh:
@@ -321,9 +333,11 @@
                 before, after = pltpu.roll(value, 1, 1), pltpu.roll(value, width - 1, 1)
             else:
                 before, after = pad[0, :, lanes].astype(F32), pad[2, :, lanes].astype(F32)
-            pad[0, :, lanes] = jnp.where(lane == 0, bring(0, line, True), before).astype(BF16)
+            pad[0, :, lanes] = jnp.where(
+                lane == 0, bring(side_map, 0, line, True), before
+            ).astype(BF16)
             pad[2, :, lanes] = jnp.where(
-                lane == width - 1, bring(1, line, False), after
+                lane == width - 1, bring(side_map, 1, line, False), after
             ).astype(BF16)
 
     def window(pad, tap, start, size):
@@ -338,11 +352,7 @@
     for r in range(height):
         put(xpad, r + 1, tall[line_of(r), :])
     edges(xpad, xedge)
-    pl.semaphore_wait(barrier, (nrow - 1) + (nwide - 1) + 4)
-    halo_copies(xpad, xedge, xrows, xside, 0)
-
-    for load in loads[3:]:
-        load.wait()
+    loads[3].wait()
     kpad[...] = jnp.zeros_like(kpad)
     kpad[: 9 * gwidth] = kern[...]
     own_group = (iota((chans, chans), 0) // gwidth) == (iota((chans, chans), 1) // gwidth)
@@ -356,31 +366,59 @@
     def _(tap):
         dense = jnp.where(own_group, mm(kpad[...], pick(tap), TN), 0.0)
         kst[:, pl.ds(pl.multiple_of(tap * chans, chans), chans)] = dense.astype(BF16)
-        other = jnp.where(own_group, mm(pick(tap), kpad[...], TN), 0.0)
-        ktst[:, pl.ds(pl.multiple_of((8 - tap) * chans, chans), chans)] = other.astype(BF16)
-
-    conv[chans:] = jnp.ones((128, cells), BF16)
-    loads[1].wait()
-    loads[2].wait()
-    tall[...] = cot[...].astype(F32).reshape(chans * height, width)
-    for r in range(height):
-        cot2[:, r * width : (r + 1) * width] = tall[line_of(r), :].astype(BF16)
-
-    @pl.loop(0, nblk)
-    def _(n):
-        lanes = pl.ds(pl.multiple_of(n * block, block), block)
-        dact[:, lanes] = mm(mix[...], cot2[:, lanes], TN)
-
-    for wait in halo_waits(xrows, xside, 0):
-        wait.wait_recv()
-
-    patch(xrows, xside, xpad, False)
+
+    for edge_tile in (slice(0, width), slice(width + cells, 2 * width + cells)):
+        xpad[:, :, edge_tile] = jnp.zeros((3, chans, width), BF16)
+    pl.semaphore_wait(barrier, (nrow - 1) + (nwide - 1) + 4)
+    halo_copies(xpad, xedge, xrows, xside, 0)
 
     @pl.loop(0, nblk)
     def _(n):
         lanes = pl.ds(pl.multiple_of(n * block, block), block)
         taps = [window(xpad, tap, n * block, block) for tap in range(9)]
-        conv[:chans, lanes] = mm(kst[...], jnp.concatenate(taps, axis=0)).astype(BF16)
+        alone[:, lanes] = mm(kst[...], jnp.concatenate(taps, axis=0))
+
+    conv[chans:] = jnp.ones((128, cells), BF16)
+    for wait in halo_waits(xrows, xside, 0):
+        wait.wait_recv()
+
+    side_map1 = side_lanes(xside)
+    put_ends(xrows, side_map1, xpad)
+    half = width // 2
+    first_cols, last_cols = [], []
+    for shift_row in range(3):
+        for at, base, found in (
+            (lane, height, first_cols),
+            (lane - half, edge_rows - half, last_cols),
+        ):
+            source = at + shift_row - 1
+            inside = jnp.logical_and(jnp.logical_and(at >= 0, at < height), source >= 0)
+            inside = jnp.logical_and(inside, source < height)
+            moved = pltpu.roll(side_map1, -(base + shift_row - 1) % width, 1)
+            found.append(jnp.where(inside, moved, 0.0).astype(BF16))
+
+    def weights(*taps):
+        return jnp.concatenate([kst[:, tap * chans : (tap + 1) * chans] for tap in taps], axis=1)
+
+    def end_rows(tile):
+        lanes = slice(tile * width, (tile + 1) * width)
+        return jnp.concatenate([xpad[which, :, lanes] for which in range(3)], axis=0)
+
+    upper = mm(weights(0, 1, 2), end_rows(0))
+    lower = mm(weights(6, 7, 8), end_rows(height + 1))
+    columns = mm(weights(0, 3, 6, 2, 5, 8), jnp.concatenate(first_cols + last_cols, axis=0))
+    for r in range(height):
+        lanes = slice(r * width, (r + 1) * width)
+        value = alone[:, lanes]
+        if r == 0:
+            value = value + upper
+        if r == height - 1:
+            value = value + lower
+        value = value + jnp.where(lane == 0, pltpu.roll(columns, -r % width, 1), 0.0)
+        value = value + jnp.where(
+            lane == width - 1, pltpu.roll(columns, (half - 1 - r) % width, 1), 0.0
+        )
+        conv[:chans, lanes] = value.astype(BF16)
 
     def all_scattered(red, recv):
         return whole(recv, nrow - 1, rs_s.at[red], rs_r.at[red])
@@ -489,6 +527,16 @@
             mrow[j : j + 1] = (mrecv if over_row else mcrecv)[red, j]
         return mrow[:count]
 
+    def planes_copy(k, slot):
+        return pltpu.make_async_remote_copy(
+            src_ref=mplane,
+            dst_ref=mblock.at[slot],
+            send_sem=mc_s.at[0],
+            recv_sem=mc_r.at[0],
+            device_id=col_peer(k),
+            device_id_type=MESH,
+        )
+
     def row_sums(source):
         return mm(jnp.ones((16, cells), BF16), source, NT)[:1]
 
@@ -496,23 +544,44 @@
         sums = jnp.concatenate([both[:, chans:]] * (chans // 128), axis=1)
         return both[:, :chans] - sums * line
 
-    local_mean = row_sums(conv[:chans]) * (1.0 / cells)
+    raw = mm(conv[: chans + 16], conv[...], NT)
+    local_mean = raw[chans : chans + 1, :chans] * (1.0 / cells)
+    scatter_start(0, send1, recv1, centred(raw[:chans], local_mean))
     spread_start(0, True, local_mean)
-    scatter_start(0, send1, recv1, centred(mm(conv[:chans], conv[...], NT), local_mean))
-    plane = spread_wait(0, True)
-    plane_mean = jnp.sum(plane, axis=0, keepdims=True) * (1.0 / nrow)
-    spread_start(0, False, plane_mean)
-    between[...] = gram(plane - plane_mean) * float(cells)
-    mine = pl.ds(pl.multiple_of(row * chunk, chunk), chunk)
-    partial = scatter_wait(0, send1, recv1) + between[mine]
-    exchange_start(0, csend1, crecv1, False, partial)
+    for load in loads[4:]:
+        load.wait()
+
+    @pl.loop(0, 9)
+    def _(tap):
+        other = jnp.where(own_group, mm(pick(tap), kpad[...], TN), 0.0)
+        ktst[:, pl.ds(pl.multiple_of((8 - tap) * chans, chans), chans)] = other.astype(BF16)
+
+    loads[1].wait()
+    loads[2].wait()
+    tall[...] = cot[...].astype(F32).reshape(chans * height, width)
+    for r in range(height):
+        cot2[:, r * width : (r + 1) * width] = tall[line_of(r), :].astype(BF16)
+
+    exchange_start(0, csend1, crecv1, False, scatter_wait(0, send1, recv1))
+    mplane[...] = spread_wait(0, True)
+    for k in range(ncol - 1):
+        planes_copy(k, col).start()
+    mblock[col] = mplane[...]
     gather_start(0, cov, exchange_wait(0, csend1, crecv1, False))
-    planes = spread_wait(0, False)
-    mean = jnp.sum(planes, axis=0, keepdims=True) * (1.0 / ncol)
+    whole(mblock, ncol - 1, mc_s.at[0], mc_r.at[0]).wait_recv()
+    means = mblock[...].reshape(nrow * ncol, chans)
+    mean = jnp.sum(means, axis=0, keepdims=True) * (1.0 / (nrow * ncol))
+    between[...] = gram(means - mean) * float(cells)
     diag = eye_mask(chans)
-    between[...] = gram(planes - mean) * float(cells * nrow)
     gain_col = to_col(gain[...])
     bias_col = to_col(bias[...])
+    put_columns(side_map1, xpad, False)
+
+    @pl.loop(0, nblk)
+    def _(n):
+        lanes = pl.ds(pl.multiple_of(n * block, block), block)
+        dact[:, lanes] = mm(mix[...], cot2[:, lanes], TN)
+
     gather_wait(0, cov)
 
     covariance = (cov[...].astype(F32) + between[...]) * (1.0 / total) + jnp.where(diag, EPS, 0.0)
@@ -520,15 +589,20 @@
     inv_trace = 1.0 / trace
     inv_root = lax.rsqrt(trace)
     normal = covariance * inv_trace
-    normal2 = mm3(normal, normal)
+    normal_r = right(normal)
+    normal2 = mm(left(normal), normal_r)
     projs = [jnp.where(diag, 1.5, 0.0) - 0.5 * normal]
-    squares = [jnp.where(diag, 2.25, 0.0) - 1.5 * normal + 0.25 * normal2]
-    mixes = [1.5 * normal - 0.5 * normal2]
+    squares = [left(jnp.where(diag, 2.25, 0.0) - 1.5 * normal + 0.25 * normal2)]
+    mixes = [right(1.5 * normal - 0.5 * normal2)]
+    projs_l, projs_r = [None], [None]
     for k in range(1, NEWTON):
         if k > 1:
-            squares.append(mm3(projs[-1], projs[-1]))
-            mixes.append(mm3(projs[-1], normal))
-        projs.append(1.5 * projs[-1] - 0.5 * mm3(squares[-1], mixes[-1]))
+            projs_l.append(left(projs[-1]))
+            projs_r.append(right(projs[-1]))
+            both = mm(projs_l[-1], jnp.concatenate([projs_r[-1], normal_r], axis=1))
+            squares.append(left(both[:, :chans]))
+            mixes.append(right(both[:, chans:]))
+        projs.append(1.5 * projs[-1] - 0.5 * mm(squares[-1], mixes[-1]))
     whiten = projs[-1] * inv_root
     wmean = jnp.sum(whiten * mean, axis=1, keepdims=True)
     whigh, wlow = split(whiten)
@@ -562,12 +636,12 @@
             added = added + xpad[1, :, (r + 1) * width : (r + 2) * width].astype(F32)
             tall[line_of(r), :] = added
 
+    exchange_start(1, csend2, crecv2, False, scatter_wait(1, send2, recv2))
     spread_start(1, False, jnp.sum(spread_wait(1, True), axis=0, keepdims=True))
-    exchange_start(1, csend2, crecv2, False, scatter_wait(1, send2, recv2))
     mixed_out[...] = tall[...].reshape(chans, height, width).astype(BF16)
     send3[...] = mm(cot2[...], act[...], NT).astype(BF16).reshape(send3.shape)
+    gather_start(1, white, exchange_wait(1, csend2, crecv2, False))
     grad_sum = jnp.sum(spread_wait(1, False), axis=0, keepdims=True)
-    gather_start(1, white, exchange_wait(1, csend2, crecv2, False))
     wsum = jnp.sum(whiten * grad_sum, axis=1, keepdims=True) * (1.0 / total)
     gain_sum = jnp.sum(gacc[...], axis=1, keepdims=True)
     bias_sum = jnp.sum(bacc[...], axis=1, keepdims=True)
@@ -577,33 +651,37 @@
     dwhiten = white[...].astype(F32)
     gwhite_out[...] = dwhiten * (1.0 / float(total) ** 0.5)
     sym = 0.5 * (dwhiten + dwhiten.T)
-    cross = mm3(sym, normal)
+    sym_r = right(sym)
+    cross = mm(left(sym), normal_r)
     dproj = -0.5 * sym
+    sym_products = mm(jnp.concatenate(projs_l[1:], axis=0), sym_r)
     for k in range(NEWTON - 1):
         if k == 0:
             dsquare = -0.75 * sym + 0.25 * cross
             dmix = 1.5 * sym - 0.5 * (cross + cross.T)
         else:
-            dsquare = mm3(dproj, projs[k])
-            dmix = mm3(dproj, normal) + mm3(projs[k], sym)
+            both = mm(left(dproj), jnp.concatenate([projs_r[k], normal_r], axis=1))
+            dsquare = both[:, :chans]
+            dmix = both[:, chans:] + sym_products[(k - 1) * chans : k * chans]
         dsquare = dsquare + dsquare.T
-        dproj = 1.5 * dproj - 0.5 * (mm3(dsquare, mixes[k]) + mm3(squares[k], dmix))
+        change = mm(
+            jnp.concatenate([left(dsquare), squares[k]], axis=1),
+            jnp.concatenate([mixes[k], right(dmix)], axis=0),
+        )
+        dproj = 1.5 * dproj - 0.5 * change
 
     scalar = full_sum(sym * projs[-1]) * 0.5 + full_sum(dproj * normal)
     dsym = inv_trace * inv_root * (dproj - jnp.where(diag, scalar, 0.0))
     dsym = (dsym + dsym.T) * (1.0 / total)
-    exchange_start(2, csend3, crecv3, True, scatter_wait(2, send3, recv3))
-
     shift_col = wsum + jnp.sum(dsym * mean, axis=1, keepdims=True)
     dhigh, dlow = split(dsym)
     quad = jnp.concatenate([whigh, wlow, dhigh, dlow], axis=1)
 
-    @pl.loop(0, nblk)
-    def _(n):
-        lanes = pl.ds(pl.multiple_of(n * block, block), block)
+    for n in range(nblk):
+        lanes = slice(n * block, (n + 1) * block)
         one, two = dnorm[:, lanes], conv[:chans, lanes]
         value = mm(quad, jnp.concatenate([one, one, two, two], axis=0)) - shift_col
-        dpad[1, :, pl.ds(pl.multiple_of(n * block + width, width), block)] = value.astype(BF16)
+        dpad[1, :, n * block + width : (n + 1) * block + width] = value.astype(BF16)
 
     turned = dpad[1, :, middle].T
 
@@ -620,11 +698,15 @@
     scale = 1.0 / float(ndp * total) ** 0.5
     edges(dpad, dedge)
     halo_copies(dpad, dedge, drows, dside, 4)
+    exchange_start(2, csend3, crecv3, True, scatter_wait(2, send3, recv3))
     exchange_start(3, csend4, crecv4, True, scatter_wait(3, send4, recv4))
-    gather_start(2, gmix, exchange_wait(2, csend3, crecv3, True) * scale)
     for wait in halo_waits(drows, dside, 4):
         wait.wait_recv()
-    patch(drows, dside, dpad, True)
+    side_map2 = side_lanes(dside)
+    put_ends(drows, side_map2, dpad)
+    put_columns(side_map2, dpad, True)
+
+    gather_start(2, gmix, exchange_wait(2, csend3, crecv3, True) * scale)
 
     def back(n):
         lanes = pl.ds(pl.multiple_of(n * block, block), block)
@@ -653,9 +735,10 @@
         all_exchanged(red, crecv).wait_send()
         if red < 3:
             all_gathered(red, full).wait_send()
-    for red in range(2):
-        all_spread(red, True).wait_send()
-        all_spread(red, False).wait_send()
+    all_spread(0, True).wait_send()
+    all_spread(1, True).wait_send()
+    all_spread(1, False).wait_send()
+    whole(mblock, ncol - 1, mc_s.at[0], mc_r.at[0]).wait_send()
 
     gather_wait(2, gmix)
     gmix_out[...] = gmix[...].astype(F32)
@@ -741,6 +824,7 @@
                 pltpu.VMEM((8, 2 * height, chans), BF16),
                 pltpu.VMEM((chans + 128, cells), BF16),
                 pltpu.VMEM((chans, cells), F32),
+                pltpu.VMEM((chans, cells), F32),
                 pltpu.VMEM((chans, cells), BF16),
                 pltpu.VMEM((chans, cells), BF16),
                 pltpu.VMEM((chans, 128), F32),
@@ -749,6 +833,8 @@
                 pltpu.VMEM((chans // 128, group_kernel.shape[1], 128), F32),
                 pltpu.VMEM((chans, chans), F32),
                 pltpu.VMEM((max(nrow, ncol), chans), F32),
+                pltpu.VMEM((nrow, chans), F32),
+                pltpu.VMEM((ncol, nrow, chans), F32),
                 pltpu.VMEM((2, 1, chans), F32),
                 pltpu.VMEM((2, nrow, 1, chans), F32),
                 pltpu.VMEM((2, 1, chans), F32),

time: 76.5 us -> 71.6 us (0.936)
  Pallas kernels: 75.7 us -> 70.8 us
    pallas_call x1, Pallas kernels: 74.5 us -> 69.6 us  [local(): pl.pallas_call(functools.partial(kernel, (ndp, nrow, ncol, height, width)...]
where the time goes in v4:
time: 71.6 us; the launch traced here: 71.5 us
  Pallas kernels  70.8 us (99%)
    pallas_call x1, Pallas kernels, local(): pl.pallas_call(functools.partial(kernel, (ndp, nrow, ncol, height, width)...  69.6 us

profile of v4, /device:TPU:1, one launch (start us, length us, event | category | flops | bytes accessed | tf_op | source)
XLA Modules:
  0.0 71.5 jit_solution(5101459924196128337)
XLA Ops:
  0.6 69.6 %shard_map.117 = (bf16[256,8,128]{2,1,0:T(8,128)(2,1)S(1)}, bf16[256,8,128]{2,1,0:T(8,128)(2,1)S(1)}, f32[256,256]{1,0:T(8,128)S(1)}, f32[1,256]{1,0:T(1,128)S(1...) custom-call(bf16[256,8,128]{2,1,0:T(8,128)(2,1)} %bitcast.11, bf16[72,256]{1,0:T(8,128)(2,1)} %bitcast.13, ...), custom_call_target="tpu_custom_call" | custom-call | tf_op jit(solution)/shard_map/pallas_call | solution.py:800
  70.2 1.2 %shard_map.118 = (bf16[256,8,128]{2,1,0:T(8,128)(2,1)}, bf16[256,8,128]{2,1,0:T(8,128)(2,1)}, f32[256,256]{1,0:T(8,128)}, f32[1,256]{1,0:T(1,128)}, f32[1,256]{1...) custom-call(bf16[256,8,128]{2,1,0:T(8,128)(2,1)S(1)} %get-tuple-element.21.refs_0_, ...), custom_call_target="tpu_custom_call" | custom-call | tf_op jit(solution)/shard_map/pallas_call | solution.py:862

commit v5 on v4

--- a/solution.py
+++ b/solution.py
@@ -211,8 +211,8 @@
         pltpu.make_async_copy(source, target, in_sems.at[i])
         for i, (source, target) in enumerate(arguments)
     ]
-    for load in loads:
-        load.start()
+    for i in (3, 0, 1, 2, 4, 5):
+        loads[i].start()
     def whole(ref, count, send_sem, recv_sem):
         part = ref.at[pl.ds(0, count)]
         return pltpu.make_async_remote_copy(
@@ -255,6 +255,17 @@
 
     def halo_copies(source, edge, rows, sides, base):
         copies = []
+        for slot, step in reversed(tuple(enumerate(SIDES))):
+            copies.append(
+                pltpu.make_async_remote_copy(
+                    src_ref=edge,
+                    dst_ref=sides.at[slot],
+                    send_sem=hsems.at[base + 2],
+                    recv_sem=hsems.at[base + 3],
+                    device_id=side_peer((-step[0], -step[1])),
+                    device_id_type=MESH,
+                )
+            )
         for slot, (step, lanes) in enumerate(
             (((1, 0), pl.ds(cells, width)), ((-1, 0), pl.ds(width, width)))
         ):
@@ -265,17 +276,6 @@
                     send_sem=hsems.at[base],
                     recv_sem=hsems.at[base + 1],
                     device_id=side_peer(step),
-                    device_id_type=MESH,
-                )
-            )
-        for slot, step in enumerate(SIDES):
-            copies.append(
-                pltpu.make_async_remote_copy(
-                    src_ref=edge,
-                    dst_ref=sides.at[slot],
-                    send_sem=hsems.at[base + 2],
-                    recv_sem=hsems.at[base + 3],
-                    device_id=side_peer((-step[0], -step[1])),
                     device_id_type=MESH,
                 )
             )
@@ -347,28 +347,28 @@
     def line_of(index):
         return pl.ds(index, chans, stride=height)
 
+    loads[3].wait()
+    kpad[...] = jnp.zeros_like(kpad)
+    kpad[: 9 * gwidth] = kern[...]
+    own_group = (iota((chans, chans), 0) // gwidth) == (iota((chans, chans), 1) // gwidth)
+
+    def pick(tap):
+        tapcol = iota((128, chans), 0)
+        within = lax.rem(iota((128, chans), 1), gwidth)
+        return (tapcol == 9 * within + tap).astype(F32).astype(BF16)
+
+    @pl.loop(0, 9)
+    def _(tap):
+        dense = jnp.where(own_group, mm(kpad[...], pick(tap), TN), 0.0)
+        kst[:, pl.ds(pl.multiple_of(tap * chans, chans), chans)] = dense.astype(BF16)
+
+    for edge_tile in (slice(0, width), slice(width + cells, 2 * width + cells)):
+        xpad[:, :, edge_tile] = jnp.zeros((3, chans, width), BF16)
     loads[0].wait()
     tall[...] = feat[...].astype(F32).reshape(chans * height, width)
     for r in range(height):
         put(xpad, r + 1, tall[line_of(r), :])
     edges(xpad, xedge)
-    loads[3].wait()
-    kpad[...] = jnp.zeros_like(kpad)
-    kpad[: 9 * gwidth] = kern[...]
-    own_group = (iota((chans, chans), 0) // gwidth) == (iota((chans, chans), 1) // gwidth)
-
-    def pick(tap):
-        tapcol = iota((128, chans), 0)
-        within = lax.rem(iota((128, chans), 1), gwidth)
-        return (tapcol == 9 * within + tap).astype(F32).astype(BF16)
-
-    @pl.loop(0, 9)
-    def _(tap):
-        dense = jnp.where(own_group, mm(kpad[...], pick(tap), TN), 0.0)
-        kst[:, pl.ds(pl.multiple_of(tap * chans, chans), chans)] = dense.astype(BF16)
-
-    for edge_tile in (slice(0, width), slice(width + cells, 2 * width + cells)):
-        xpad[:, :, edge_tile] = jnp.zeros((3, chans, width), BF16)
     pl.semaphore_wait(barrier, (nrow - 1) + (nwide - 1) + 4)
     halo_copies(xpad, xedge, xrows, xside, 0)
 
@@ -671,8 +671,7 @@
         dproj = 1.5 * dproj - 0.5 * change
 
     scalar = full_sum(sym * projs[-1]) * 0.5 + full_sum(dproj * normal)
-    dsym = inv_trace * inv_root * (dproj - jnp.where(diag, scalar, 0.0))
-    dsym = (dsym + dsym.T) * (1.0 / total)
+    dsym = (inv_trace * inv_root * (2.0 / total)) * (dproj - jnp.where(diag, scalar, 0.0))
     shift_col = wsum + jnp.sum(dsym * mean, axis=1, keepdims=True)
     dhigh, dlow = split(dsym)
     quad = jnp.concatenate([whigh, wlow, dhigh, dlow], axis=1)

time: 71.6 us -> 71.5 us (level)
  no operation moved by 1% of the time
where the time goes in v5:
time: 71.5 us; the launch traced here: 71.4 us
  Pallas kernels  70.6 us (99%)
  between operations  0.8 us (1%)
    pallas_call x1, Pallas kernels, local(): pl.pallas_call(functools.partial(kernel, (ndp, nrow, ncol, height, width)...  69.4 us

profile of v5, /device:TPU:1, one launch (start us, length us, event | category | flops | bytes accessed | tf_op | source)
XLA Modules:
  0.0 71.4 jit_solution(9150831929737870768)
XLA Ops:
  0.6 69.4 %shard_map.117 = (bf16[256,8,128]{2,1,0:T(8,128)(2,1)S(1)}, bf16[256,8,128]{2,1,0:T(8,128)(2,1)S(1)}, f32[256,256]{1,0:T(8,128)S(1)}, f32[1,256]{1,0:T(1,128)S(1...) custom-call(bf16[256,8,128]{2,1,0:T(8,128)(2,1)} %bitcast.11, bf16[72,256]{1,0:T(8,128)(2,1)} %bitcast.13, ...), custom_call_target="tpu_custom_call" | custom-call | tf_op jit(solution)/shard_map/pallas_call | solution.py:799
  70.0 1.2 %shard_map.118 = (bf16[256,8,128]{2,1,0:T(8,128)(2,1)}, bf16[256,8,128]{2,1,0:T(8,128)(2,1)}, f32[256,256]{1,0:T(8,128)}, f32[1,256]{1,0:T(1,128)}, f32[1,256]{1...) custom-call(bf16[256,8,128]{2,1,0:T(8,128)(2,1)S(1)} %get-tuple-element.21.refs_0_, ...), custom_call_target="tpu_custom_call" | custom-call | tf_op jit(solution)/shard_map/pallas_call | solution.py:861
